TPU v7x, 32 devices: a whole 2x2x4 slice. The times are simulated.
32 devices in a mesh: gx: 4 (over z), gy: 8 (over y, x, core).
Axes of the slice: x: 2, y: 2, z: 4, core: 2. Of those that a mesh axis runs over, the one named last changes fastest.
Arguments:
- coeffs: bfloat16 [8, 64, 256, 128], P('gx', 'gy'), may hold values from -0.25 to 0.25
- permit: float32 [8, 64, 256], P('gx', 'gy'), may hold values from 0.25 to 4
- shift_diag: float32 [8, 64, 128], P('gx', 'gy'), may hold values from 0.5 to 4
- codes: int32 [8, 64, 6], P('gx', 'gy'), may hold values from 0 to 8
- counts: int32 [8, 64], P('gx', 'gy'), may hold values from 1 to 6
- weights: float32 [8, 64, 6], P('gx', 'gy'), may hold values from 0.5 to 1.5
- vectors: bfloat16 [8, 64, 128, 128], P('gx', 'gy'), may hold values from -6 to 6
Outputs:
- factor: bfloat16 [8, 64, 128, 128], P('gx', 'gy')
- applied: bfloat16 [8, 64, 128, 128], P('gx', 'gy')
All inputs are finite; a program needn't handle non-finite values.
Results may differ from a plain program's by a relative error of at most 0.0051.
Values may be sent and summed in bfloat16 or wider, within the bound.
A program may use at most 64 MiB of HBM per device.

v0:
```python
import jax
import jax.numpy as jnp
from jax import lax
from jax.sharding import PartitionSpec as P


def extended(block, sides, width):
    for axis, dim in sides:
        count = lax.axis_size(axis)
        forward = [(i, i + 1) for i in range(count - 1)]
        backward = [(target, source) for source, target in forward]
        low = lax.ppermute(
            lax.slice_in_dim(block, block.shape[dim] - width, None, axis=dim), axis, forward
        )
        high = lax.ppermute(lax.slice_in_dim(block, 0, width, axis=dim), axis, backward)
        block = jnp.concatenate([low, block, high], axis=dim)
    return block


def local(coeffs, permit, shift_diag, codes, counts, weights, vectors):
    blocks_x = coeffs.shape[0]
    blocks_y = coeffs.shape[1]
    coupling = coeffs.shape[2]
    order = coeffs.shape[3]
    slots = codes.shape[2]
    padded = extended(coeffs, (("gx", 0), ("gy", 1)), 1)
    flattened = padded.reshape((blocks_x + 2) * (blocks_y + 2), coupling, order)
    row_index = jnp.arange(blocks_x, dtype=jnp.int32)[:, None]
    column_index = jnp.arange(blocks_y, dtype=jnp.int32)[None, :]
    active = jnp.arange(slots)[None, None, :] < counts[:, :, None]
    gram = jnp.zeros((blocks_x, blocks_y, order, order), jnp.float32)
    for slot_num in range(slots):
        slot_code = codes[:, :, slot_num]
        flat_index = (row_index + slot_code // 3) * (blocks_y + 2) + column_index + slot_code % 3
        neighbour = jnp.take(flattened, flat_index.reshape(-1), axis=0).reshape(
            blocks_x, blocks_y, coupling, order
        )
        scaled = (permit[:, :, :, None] * neighbour).astype(jnp.bfloat16)
        product = jnp.einsum(
            "xyrk,xyrl->xykl", scaled, neighbour, preferred_element_type=jnp.float32
        )
        gram = gram + jnp.where(active[:, :, slot_num, None, None], product, jnp.float32(0.0))
    system = gram + shift_diag[:, :, :, None] * jnp.eye(order, dtype=jnp.float32)
    cholesky_factor = jnp.linalg.cholesky(system)
    identity = jnp.broadcast_to(jnp.eye(order, dtype=system.dtype), system.shape)
    inverse = lax.linalg.triangular_solve(cholesky_factor, identity, left_side=True, lower=True)
    factor = inverse.astype(jnp.bfloat16)
    images = jnp.einsum("xykl,xykv->xylv", factor, vectors, preferred_element_type=jnp.float32)
    width_v = vectors.shape[3]
    weight_list = []
    for offset in range(9):
        weight_list.append(
            jnp.sum(jnp.where(active & (codes == offset), weights, jnp.float32(0.0)), axis=-1)
        )
    stacked = jnp.stack(weight_list, axis=-1)
    nearby, nearby_weights = (
        extended(images, (("gx", 0), ("gy", 1)), 1),
        extended(stacked, (("gx", 0), ("gy", 1)), 1),
    )
    total = jnp.zeros((blocks_x, blocks_y, order, width_v), jnp.float32)
    for offset in range(9):
        along_x = offset // 3
        along_y = offset % 3
        weight_here = nearby_weights[
            along_x : along_x + blocks_x, along_y : along_y + blocks_y, 8 - offset
        ]
        total = (
            total
            + weight_here[:, :, None, None]
            * nearby[along_x : along_x + blocks_x, along_y : along_y + blocks_y]
        )
    applied = total.astype(jnp.bfloat16)
    return (factor, applied)


def solution(mesh):
    placed = (
        P("gx", "gy", None, None),
        P("gx", "gy", None),
        P("gx", "gy", None),
        P("gx", "gy", None),
        P("gx", "gy"),
        P("gx", "gy", None),
        P("gx", "gy", None, None),
    )
    return jax.shard_map(
        local,
        mesh=mesh,
        in_specs=placed,
        out_specs=(P("gx", "gy", None, None), P("gx", "gy", None, None)),
        check_vma=False,
    )
```

profile of v0, /device:TPU:4, one launch (start us, length us, event | category | flops | bytes accessed | tf_op | source)
XLA Modules:
  0.0 471.1 jit_solution(10407429515939242776)
XLA Ops:
  0.7 2.2 fusion.49
  2.9 3.5 collective-permute-start
  6.4 1.3 collective-permute-start.1
  7.7 0.8 slice_divide_fusion
  8.5 0.8 sign_compare_fusion
  9.2 0.6 fusion.27
  9.9 0.6 iota_compare_fusion.1
  10.5 0.6 iota_compare_fusion.2
  12.8 0.7 fusion.36
  13.5 0.6 compare_and_fusion.5
  14.0 0.6 compare_and_fusion
  14.6 0.6 pad_clamp_fusion.4
  15.3 0.6 pad_clamp_fusion.2
  15.9 1.9 collective-permute-done
  18.0 3.6 collective-permute-done.1
  21.7 1.3 copy-done.7
  23.1 1.9 collective-permute-start.2
  25.1 4.5 collective-permute-start.3
  29.6 0.6 pad_clamp_fusion
  30.3 0.6 slice_bitcast_fusion
  30.9 0.9 collective-permute-done.2
  31.8 1.7 collective-permute-done.3
  33.5 2.0 pad_maximum_fusion
  35.5 1.8 gather_fusion
  37.3 2.3 broadcast_select_fusion.5
  39.6 2.3 copy.27
  41.9 1.9 gather_fusion.1
  43.8 2.5 broadcast_select_fusion.4
  46.2 2.3 copy.29
  48.5 1.8 gather_fusion.2
  50.3 2.4 broadcast_select_fusion.3
  52.7 2.3 copy.31
  55.0 1.8 gather_fusion.3
  56.8 2.4 broadcast_select_fusion.2
  59.2 2.3 copy.33
  61.5 1.8 gather_fusion.4
  63.2 2.4 broadcast_select_fusion.1
  65.6 2.3 copy.35
  67.9 1.8 gather_fusion.5
  69.7 2.5 broadcast_select_fusion
  72.2 2.4 copy.37
  74.5 1.7 convolution_select_fusion.5
  76.3 0.4 fusion.4
  76.8 0.7 copy-done.3
  79.1 0.5 copy-done.5
  81.2 1.3 copy.40
  82.5 1.6 fusion.18
  84.1 1.3 copy.41
  85.4 188.3 %custom-call.7 = f32[2,8,128,128]{3,2,1,0:T(8,128)S(1)} custom-call(f32[2,8,128,128]{3,2,1,0:T(8,128)} %copy.41), custom_call_target="Cholesky" | custom-call | tf_op jit(solution)/shard_map/jit(cholesky)/cholesky | solution.py:44
  274.2 157.4 %custom-call.8 = f32[2,8,1,128,128]{3,4,2,1,0:T(8,128)S(1)} custom-call(f32[2,8,1,128,128]{4,3,2,1,0:T(8,128)S(1)} %select_bitcast_fusion), custom_call_target="InvertDiagBlocksLowerTriangular" | custom-call | tf_op jit(solution)/shard_map/triangular_solve | solution.py:46
  431.6 1.8 convolution_convert_fusion
  433.9 3.5 collective-permute-start.7
  437.4 1.3 collective-permute-start.8
  438.7 4.5 collective-permute-start.4
  443.3 1.3 collective-permute-start.5
  444.6 5.2 %collective-permute-done.4 = f32[1,8,9]{1,0,2:T(1,128)S(1)} collective-permute-done((f32[1,8,9]{1,0,2:T(1,128)S(1)}, f32[1,8,9]{1,0,2:T(1,128)S(1)}, u32[]{:S(2)}, u32[]{:S(2)}) %collective-permute-start.4) | collective-permute-done | bytes 320 | tf_op jit(solution)/shard_map/ppermute | solution.py:12
  449.7 4.2 collective-permute-done.5
  454.0 2.2 collective-permute-start.11
  456.2 2.1 collective-permute-start.9
  458.4 4.3 collective-permute-start.10
  462.7 1.9 collective-permute-start.6
  464.8 4.0 collective-permute-done.6
  468.8 0.6 maximum_maximum_fusion
  469.5 1.6 fusion.6
  (131 shorter events, 6.5 us)
Async XLA Ops:
  0.6 432.8 %copy-start = (bf16[2,8,128,128]{3,2,1,0:T(8,128)(2,1)S(1)}, bf16[2,8,128,128]{3,2,1,0:T(8,128)(2,1)}, u32[]{:S(2)}) copy-start(bf16[2,8,128,128]{3,2,1,0:T(8,128)(2,1)} %param.15) | copy-start | bytes 1572868
  0.6 17.2 %copy-start.13 = (bf16[2,8,256,128]{3,2,1,0:T(8,128)(2,1)S(1)}, bf16[2,8,256,128]{3,2,1,0:T(8,128)(2,1)}, u32[]{:S(2)}) copy-start(bf16[2,8,256,128]{3,2,1,0:T(8,128)(2,1)} %param.9) | copy-start | bytes 3145732
  0.7 12.1 %copy-start.19 = (s32[2,8,6]{1,0,2:T(2,128)S(1)}, s32[2,8,6]{1,0,2:T(2,128)}, u32[]{:S(2)}) copy-start(s32[2,8,6]{1,0,2:T(2,128)} %param.12) | copy-start | bytes 1156
  0.7 12.1 %copy-start.25 = (s32[2,8]{1,0:T(2,128)S(1)}, s32[2,8]{1,0:T(2,128)}, u32[]{:S(2)}) copy-start(s32[2,8]{1,0:T(2,128)} %param.13) | copy-start | bytes 196
  0.7 12.1 %copy-start.23 = (f32[2,8,6]{1,0,2:T(2,128)S(1)}, f32[2,8,6]{1,0,2:T(2,128)}, u32[]{:S(2)}) copy-start(f32[2,8,6]{1,0,2:T(2,128)} %param.14) | copy-start | bytes 1156
  2.9 15.0 %collective-permute-start = (bf16[1,8,256,128]{3,2,1,0:T(8,128)(2,1)}, bf16[1,8,256,128]{3,2,1,0:T(8,128)(2,1)S(1)}, u32[]{:S(2)}, u32[]{:S(2)}) collective-permute-start(bf16[1,8,256,128]{3,2,1,0:T(8,128)(2,1)} %get-tuple-element.33), channel_id=1, source_target_pairs={{0,8},{8,16},{16,24},{1,9},{9,17},{17,25},{2,10},{10,18},{18,26},{... | collective-permute-start | bytes 1572872 | tf_op jit(solution)/shard_map/ppermute | solution.py:12
  6.4 15.3 %collective-permute-start.1 = (bf16[1,8,256,128]{3,2,1,0:T(8,128)(2,1)S(1)}, bf16[1,8,256,128]{3,2,1,0:T(8,128)(2,1)S(1)}, u32[]{:S(2)}, u32[]{:S(2)}) collective-permute-start(bf16[1,8,256,128]{3,2,1,0:T(8,128)(2,1)S(1)} %get-tuple-element.32), channel_id=1, source_target_pairs={{8,0},{16,8},{24,16},{9,1},{17,9},{25,17},{10,2},{18,10},{26,18},{... | collective-permute-start | bytes 1572872 | tf_op jit(solution)/shard_map/ppermute | solution.py:15
  13.5 9.7 %copy-start.21 = (f32[2,8]{1,0:T(2,128)}, f32[2,8]{1,0:T(2,128)S(1)}, u32[]{:S(2)}) copy-start(f32[2,8]{1,0:T(2,128)S(1)} %get-tuple-element.6) | copy-start | bytes 196
  17.9 12.3 %copy-start.16 = (f32[128,128]{1,0:T(8,128)S(1)}, f32[128,128]{1,0:T(8,128)}, u32[]{:S(2)}) copy-start(f32[128,128]{1,0:T(8,128)} %fusion.27) | copy-start | bytes 196612
  21.7 1.3 copy-start.7
  23.1 8.7 %collective-permute-start.2 = (bf16[4,1,256,128]{3,2,1,0:T(8,128)(2,1)S(1)}, bf16[4,1,256,128]{3,2,1,0:T(8,128)(2,1)S(1)}, u32[]{:S(2)}, u32[]{:S(2)}) collective-permute-start(bf16[4,1,256,128]{3,2,1,0:T(8,128)(2,1)S(1)} %get-tuple-element.28), channel_id=1, source_target_pairs={{0,1},{1,2},{2,3},{3,4},{4,5},{5,6},{6,7},{8,9},{9,10},{10,11},{11... | collective-permute-start | bytes 786440 | tf_op jit(solution)/shard_map/ppermute | solution.py:12
  25.1 8.4 %collective-permute-start.3 = (bf16[4,1,256,128]{3,2,1,0:T(8,128)(2,1)S(1)}, bf16[4,1,256,128]{3,2,1,0:T(8,128)(2,1)}, u32[]{:S(2)}, u32[]{:S(2)}) collective-permute-start(bf16[4,1,256,128]{3,2,1,0:T(8,128)(2,1)S(1)} %get-tuple-element.29), channel_id=1, source_target_pairs={{1,0},{2,1},{3,2},{4,3},{5,4},{6,5},{7,6},{9,8},{10,9},{11,10},{12... | collective-permute-start | bytes 786440 | tf_op jit(solution)/shard_map/ppermute | solution.py:15
  30.9 6.4 %copy-start.31 = (pred[16]{0:T(512)(128)(4,1)S(1)}, pred[16]{0:T(512)(128)(4,1)}, u32[]{:S(2)}) copy-start(pred[16]{0:T(512)(128)(4,1)} %get-tuple-element.22) | copy-start | bytes 52
  39.6 4.2 copy-start.30
  46.2 4.1 copy-start.29
  52.7 4.1 copy-start.28
  59.2 4.0 copy-start.27
  65.6 4.1 copy-start.26
  69.7 4.9 %copy-start.1 = (bf16[16,256,128]{2,1,0:T(8,128)(2,1)S(1)}, bf16[16,256,128]{2,1,0:T(8,128)(2,1)}, u32[]{:S(2)}) copy-start(bf16[16,256,128]{2,1,0:T(8,128)(2,1)} %broadcast_select_fusion.5) | copy-start | bytes 3145732
  69.7 4.9 %copy-start.15 = (f32[2,8,256]{2,1,0:T(8,128)S(1)}, f32[2,8,256]{2,1,0:T(8,128)}, u32[]{:S(2)}) copy-start(f32[2,8,256]{2,1,0:T(8,128)} %param.10) | copy-start | bytes 49156
  69.7 4.9 %copy-start.37 = (pred[2,8]{1,0:T(4,128)(4,1)S(1)}, pred[2,8]{1,0:T(4,128)(4,1)}, u32[]{:S(2)}) copy-start(pred[2,8]{1,0:T(4,128)(4,1)} %get-tuple-element.69) | copy-start | bytes 52
  72.2 4.1 copy-start.2
  72.2 4.2 copy-start.36
  74.5 1.8 copy-start.8
  76.3 1.2 copy-start.3
  76.3 1.5 copy-start.9
  76.3 1.5 copy-start.35
  76.8 1.5 copy-start.4
  76.8 1.8 copy-start.10
  76.8 1.8 copy-start.34
  78.3 1.3 copy-start.5
  78.3 1.6 copy-start.11
  78.3 1.6 copy-start.33
  79.0 1.4 copy-start.6
  79.0 1.7 copy-start.12
  79.0 1.7 copy-start.32
  80.7 1.8 copy-start.20
  82.5 191.2 %copy-start.18 = (pred[128,128]{1,0:T(8,128)(4,1)S(1)}, pred[128,128]{1,0:T(8,128)(4,1)}, u32[]{:S(2)}) copy-start(pred[128,128]{1,0:T(8,128)(4,1)} %iota_compare_fusion.1) | copy-start | bytes 49156
  84.1 189.9 %copy-start.17 = (pred[128,128]{1,0:T(8,128)(4,1)S(1)}, pred[128,128]{1,0:T(8,128)(4,1)}, u32[]{:S(2)}) copy-start(pred[128,128]{1,0:T(8,128)(4,1)} %iota_compare_fusion.2) | copy-start | bytes 49156
  433.4 20.6 %copy-start.14 = (bf16[2,8,128,128]{3,2,1,0:T(8,128)(2,1)}, bf16[2,8,128,128]{3,2,1,0:T(8,128)(2,1)S(1)}, u32[]{:S(2)}) copy-start(bf16[2,8,128,128]{3,2,1,0:T(8,128)(2,1)S(1)} %convolution_convert_fusion) | copy-start | bytes 1572868
  433.4 5.3 %copy-start.24 = (f32[2,8]{1,0:T(2,128)S(1)}, f32[2,8]{1,0:T(2,128)}, u32[]{:S(2)}) copy-start(f32[2,8]{1,0:T(2,128)} %get-tuple-element.3) | copy-start | bytes 196
  433.9 20.0 %collective-permute-start.7 = (f32[1,8,128,128]{3,2,1,0:T(8,128)S(1)}, f32[1,8,128,128]{3,2,1,0:T(8,128)S(1)}, u32[]{:S(2)}, u32[]{:S(2)}) collective-permute-start(f32[1,8,128,128]{3,2,1,0:T(8,128)S(1)} %get-tuple-element.30), channel_id=1, source_target_pairs={{0,8},{8,16},{16,24},{1,9},{9,17},{17,25},{2,10},{10,18},{18,26},{... | collective-permute-start | bytes 1572872 | tf_op jit(solution)/shard_map/ppermute | solution.py:12
  437.4 16.6 %collective-permute-start.8 = (f32[1,8,128,128]{3,2,1,0:T(8,128)S(1)}, f32[1,8,128,128]{3,2,1,0:T(8,128)S(1)}, u32[]{:S(2)}, u32[]{:S(2)}) collective-permute-start(f32[1,8,128,128]{3,2,1,0:T(8,128)S(1)} %get-tuple-element.31), channel_id=1, source_target_pairs={{8,0},{16,8},{24,16},{9,1},{17,9},{25,17},{10,2},{18,10},{26,18},{... | collective-permute-start | bytes 1572872 | tf_op jit(solution)/shard_map/ppermute | solution.py:15
  438.7 11.0 %collective-permute-start.4 = (f32[1,8,9]{1,0,2:T(1,128)S(1)}, f32[1,8,9]{1,0,2:T(1,128)S(1)}, u32[]{:S(2)}, u32[]{:S(2)}) collective-permute-start(f32[1,8,9]{1,0,2:T(1,128)S(1)} %get-tuple-element.44), channel_id=1, source_target_pairs={{0,8},{8,16},{16,24},{1,9},{9,17},{17,25},{2,10},{10,18},{18,26},{... | collective-permute-start | bytes 872 | tf_op jit(solution)/shard_map/ppermute | solution.py:12
  443.3 10.6 %collective-permute-start.5 = (f32[1,8,9]{1,0,2:T(1,128)S(1)}, f32[1,8,9]{1,0,2:T(1,128)S(1)}, u32[]{:S(2)}, u32[]{:S(2)}) collective-permute-start(f32[1,8,9]{1,0,2:T(1,128)S(1)} %get-tuple-element.45), channel_id=1, source_target_pairs={{8,0},{16,8},{24,16},{9,1},{17,9},{25,17},{10,2},{18,10},{26,18},{... | collective-permute-start | bytes 872 | tf_op jit(solution)/shard_map/ppermute | solution.py:15
  454.0 14.8 %collective-permute-start.11 = (f32[4,1,128,128]{3,2,1,0:T(8,128)S(1)}, f32[4,1,128,128]{3,2,1,0:T(8,128)S(1)}, u32[]{:S(2)}, u32[]{:S(2)}) collective-permute-start(f32[4,1,128,128]{3,2,1,0:T(8,128)S(1)} %get-tuple-element.27), channel_id=1, source_target_pairs={{1,0},{2,1},{3,2},{4,3},{5,4},{6,5},{7,6},{9,8},{10,9},{11,10},{12... | collective-permute-start | bytes 786440 | tf_op jit(solution)/shard_map/ppermute | solution.py:15
  456.2 12.6 %collective-permute-start.9 = (f32[4,1,128,128]{3,2,1,0:T(8,128)S(1)}, f32[4,1,128,128]{3,2,1,0:T(8,128)S(1)}, u32[]{:S(2)}, u32[]{:S(2)}) collective-permute-start(f32[4,1,128,128]{3,2,1,0:T(8,128)S(1)} %get-tuple-element.26), channel_id=1, source_target_pairs={{0,1},{1,2},{2,3},{3,4},{4,5},{5,6},{6,7},{8,9},{9,10},{10,11},{11... | collective-permute-start | bytes 786440 | tf_op jit(solution)/shard_map/ppermute | solution.py:12
  458.4 6.3 %collective-permute-start.10 = (f32[4,1,9]{1,0,2:T(4,128)S(1)}, f32[4,1,9]{1,0,2:T(4,128)S(1)}, u32[]{:S(2)}, u32[]{:S(2)}) collective-permute-start(f32[4,1,9]{1,0,2:T(4,128)S(1)} %get-tuple-element.41), channel_id=1, source_target_pairs={{1,0},{2,1},{3,2},{4,3},{5,4},{6,5},{7,6},{9,8},{10,9},{11,10},{12... | collective-permute-start | bytes 440 | tf_op jit(solution)/shard_map/ppermute | solution.py:15
  462.7 6.0 %collective-permute-start.6 = (f32[4,1,9]{1,0,2:T(4,128)S(1)}, f32[4,1,9]{1,0,2:T(4,128)S(1)}, u32[]{:S(2)}, u32[]{:S(2)}) collective-permute-start(f32[4,1,9]{1,0,2:T(4,128)S(1)} %get-tuple-element.40), channel_id=1, source_target_pairs={{0,1},{1,2},{2,3},{3,4},{4,5},{5,6},{6,7},{8,9},{9,10},{10,11},{11... | collective-permute-start | bytes 440 | tf_op jit(solution)/shard_map/ppermute | solution.py:12
  468.8 0.7 copy-start.22
where the time goes:
time: 472 us; the launch traced here: 471 us
  other arithmetic  374 us (79%)
  local copies, waits for them, and re-layouts  36.3 us (8%)
  starting transfers between devices  32.5 us (7%)
  waiting for transfers between devices  21.4 us (5%)
  matrix products  6.06 us (1%)
    another operation x4, other arithmetic, local(): cholesky_factor = jnp.linalg.cholesky(system)  189 us
    another operation x3, other arithmetic, local(): lax.linalg.triangular_solve(cholesky_factor, identity, left_side=True, lo...  158 us
    ppermute x6, starting transfers between devices, extended(): lax.ppermute(lax.slice_in_dim(block, block.shape[dim] - width, None, axis...  17.5 us
    ppermute x6, starting transfers between devices, extended(): lax.ppermute(lax.slice_in_dim(block, 0, width, axis=dim), axis, backward)  14.9 us
    select_n x6, other arithmetic, local(): jnp.take(flattened, flat_index.reshape(-1), axis=0)  14.4 us
    select_n x6, local copies, waits for them, and re-layouts, local(): jnp.take(flattened, flat_index.reshape(-1), axis=0)  13.7 us
    ppermute x6, waiting for transfers between devices, extended(): lax.ppermute(lax.slice_in_dim(block, block.shape[dim] - width, None, axis...  11.9 us
    gather x6, local copies, waits for them, and re-layouts, local(): jnp.take(flattened, flat_index.reshape(-1), axis=0)  10.8 us
  transfers between devices with their start and end apart: 12, of which 7 were waited for; matrix products, arithmetic and copies ran while one was open for 2% of the time, Pallas kernels for 0%

commit v1 on v0

v1 whole, which is shorter than its diff:
```python
import functools

import jax
import jax.numpy as jnp
from jax import lax
from jax.experimental import pallas as pl
from jax.experimental.pallas import tpu as pltpu
from jax.sharding import PartitionSpec as P

MESH = pl.DeviceIdType.MESH
DIRS = ((1, 0), (-1, 0), (0, 1), (0, -1), (1, 1), (1, -1), (-1, 1), (-1, -1))


def neighbours():
    sizes = (lax.axis_size("gx"), lax.axis_size("gy"))
    me = (lax.axis_index("gx"), lax.axis_index("gy"))

    def there(d):
        return (me[0] + d[0], me[1] + d[1])

    def exists(d):
        ok = None
        for size, at, step in zip(sizes, me, d):
            if step == 0:
                continue
            test = (at + 1 < size) if step > 0 else (at > 0)
            ok = test if ok is None else jnp.logical_and(ok, test)
        return ok

    return there, exists


def exchange(sends, lands, send_sem, recv_sem, before=None):
    there, exists = neighbours()
    barrier = pltpu.get_barrier_semaphore()
    for d in DIRS:
        @pl.when(exists(d))
        def _(d=d):
            pl.semaphore_signal(barrier, inc=1, device_id=there(d), device_id_type=MESH)
    near = [exists(d).astype(jnp.int32) for d in DIRS[:4]]
    pl.semaphore_wait(barrier, (near[0] + near[1] + 1) * (near[2] + near[3] + 1) - 1)

    def copy(k, d):
        return pltpu.make_async_remote_copy(
            src_ref=sends[k], dst_ref=lands[k], send_sem=send_sem.at[k], recv_sem=recv_sem.at[k],
            device_id=there(d), device_id_type=MESH)

    for k, d in enumerate(DIRS):
        @pl.when(exists(d))
        def _(k=k, d=d):
            copy(k, d).start()

    def finish():
        for k, d in enumerate(DIRS):
            @pl.when(exists((-d[0], -d[1])))
            def _(k=k, d=d):
                copy(k, d).wait_recv()
        for k, d in enumerate(DIRS):
            @pl.when(exists(d))
            def _(k=k, d=d):
                copy(k, d).wait_send()

    return finish


def halo_kernel(c_ref, hx_ref, hy_ref, hc_ref, send_sem, recv_sem):
    bx, by = c_ref.shape[0], c_ref.shape[1]
    row = {1: bx - 1, -1: 0}
    col = {1: by - 1, -1: 0}
    sends = [c_ref.at[bx - 1], c_ref.at[0], c_ref.at[:, by - 1], c_ref.at[:, 0]]
    lands = [hx_ref.at[0], hx_ref.at[1], hy_ref.at[0], hy_ref.at[1]]
    for k, d in enumerate(DIRS[4:]):
        sends.append(c_ref.at[row[d[0]], col[d[1]]])
        lands.append(hc_ref.at[k])
    exchange(sends, lands, send_sem, recv_sem)()


def factor_kernel(c_ref, hx_ref, hy_ref, hc_ref, permit_ref, shift_ref, codes_ref, counts_ref, weights_ref,
                  v_ref, fac_ref, loc_ref, px_ref, py_ref, pc_ref, cs, ts, gs, ss, sem):
    bx, by, coupling, order = c_ref.shape
    slots = codes_ref.shape[2]
    blocks = bx * by
    wide = by + 2
    nx, ny = lax.axis_size("gx"), lax.axis_size("gy")
    gx, gy = lax.axis_index("gx"), lax.axis_index("gy")
    moves = []
    for x in range(bx):
        moves.append((c_ref.at[x], cs.at[pl.ds((x + 1) * wide + 1, by)]))
        moves.append((hy_ref.at[0, x], cs.at[(x + 1) * wide]))
        moves.append((hy_ref.at[1, x], cs.at[(x + 1) * wide + by + 1]))
    moves.append((hx_ref.at[0], cs.at[pl.ds(1, by)]))
    moves.append((hx_ref.at[1], cs.at[pl.ds((bx + 1) * wide + 1, by)]))
    moves.append((hc_ref.at[0], cs.at[0]))
    moves.append((hc_ref.at[1], cs.at[by + 1]))
    moves.append((hc_ref.at[2], cs.at[(bx + 1) * wide]))
    moves.append((hc_ref.at[3], cs.at[(bx + 1) * wide + by + 1]))
    copies = [pltpu.make_async_copy(a, b, sem.at[k]) for k, (a, b) in enumerate(moves)]
    for copy in copies:
        copy.start()

    @pl.loop(0, (bx + 2) * wide)
    def _(n):
        ss[n] = jnp.zeros(ss.shape[1:], ss.dtype)

    for copy in copies:
        copy.wait()

    @pl.loop(0, (bx + 2) * wide)
    def _(n):
        ts[n] = cs[n].T

    def slot_at(x, y, s):
        code = codes_ref[x, y, s]
        ax, ay = code // 3, code % 3
        whole_x, whole_y = gx * bx + x + ax - 1, gy * by + y + ay - 1
        ok = (s < counts_ref[x, y]) & (whole_x >= 0) & (whole_x < nx * bx) & (whole_y >= 0) & (whole_y < ny * by)
        return jnp.where(ok, (x + ax) * wide + y + ay, (x + 1) * wide + y + 1), ok

    rows = lax.broadcasted_iota(jnp.int32, (order, order), 0)
    lanes = lax.broadcasted_iota(jnp.int32, (order, order), 1)

    @pl.loop(0, blocks)
    def _(i):
        x, y = i // by, i % by
        p = permit_ref[x, pl.ds(y, 1), :]
        acc = jnp.zeros((order, order), jnp.float32)
        for s in range(slots):
            n, ok = slot_at(x, y, s)
            scaled = (ts[n].astype(jnp.float32) * jnp.where(ok, p, 0.0)).astype(jnp.bfloat16)
            acc = acc + jnp.dot(scaled, cs[n], preferred_element_type=jnp.float32)
        gs[i] = 0.5 * (acc + acc.T) + jnp.where(rows == lanes, shift_ref[x, pl.ds(y, 1), :], 0.0)

    parts = 4
    step = order // parts
    for part in range(parts):
        low = part * step
        height = order - low
        row_here = lax.broadcasted_iota(jnp.int32, (height, order), 0) + low
        lane_row = lax.broadcasted_iota(jnp.int32, (1, order), 1)

        @pl.loop(low, low + step)
        def _(k):
            below = row_here > k
            pick = jnp.full((height, order), k, jnp.int32)
            for b in range(blocks):
                m = gs[b, low:, :]
                r = gs[b, pl.ds(k, 1), :]
                d = jnp.sum(jnp.where(lane_row == k, r, 0.0), axis=1, keepdims=True)
                r = (r + jnp.where(lane_row == k, 1.0, 0.0)) / d
                f = jnp.where(below, jnp.take_along_axis(m, pick, axis=1), 0.0)
                gs[b, low:, :] = m - f * r

    @pl.loop(0, blocks)
    def _(i):
        x, y = i // by, i % by
        m = gs[i]
        d = jnp.sum(jnp.where(rows == lanes, m, 0.0), axis=1, keepdims=True)
        inverse = jnp.where(rows > lanes, m, jnp.where(rows == lanes, 1.0, 0.0)) * lax.rsqrt(d)
        factor = inverse.astype(jnp.bfloat16)
        fac_ref[x, y] = factor
        image = lax.dot_general(factor, v_ref[x, y], (((0,), (0,)), ((), ())), preferred_element_type=jnp.float32)
        for s in range(slots):
            n, ok = slot_at(x, y, s)
            w = jnp.where(ok, weights_ref[x, y, s], 0.0)
            ss[n] = ss[n] + w * image

    for x in range(bx):
        for y in range(by):
            loc_ref[x, y] = ss[(x + 1) * wide + y + 1]
        py_ref[1, x] = ss[(x + 1) * wide].astype(jnp.bfloat16)
        py_ref[0, x] = ss[(x + 1) * wide + by + 1].astype(jnp.bfloat16)
    for y in range(by):
        px_ref[1, y] = ss[y + 1].astype(jnp.bfloat16)
        px_ref[0, y] = ss[(bx + 1) * wide + y + 1].astype(jnp.bfloat16)
    pc_ref[0] = ss[(bx + 1) * wide + by + 1].astype(jnp.bfloat16)
    pc_ref[1] = ss[(bx + 1) * wide].astype(jnp.bfloat16)
    pc_ref[2] = ss[by + 1].astype(jnp.bfloat16)
    pc_ref[3] = ss[0].astype(jnp.bfloat16)


def sum_kernel(loc_ref, px_ref, py_ref, pc_ref, out_ref, rx, ry, rc, send_sem, recv_sem):
    bx, by = loc_ref.shape[0], loc_ref.shape[1]
    _, exists = neighbours()
    sends = [px_ref.at[0], px_ref.at[1], py_ref.at[0], py_ref.at[1]] + [pc_ref.at[k] for k in range(4)]
    lands = [rx.at[0], rx.at[1], ry.at[0], ry.at[1]] + [rc.at[k] for k in range(4)]
    for k, d in enumerate(DIRS):
        @pl.when(jnp.logical_not(exists((-d[0], -d[1]))))
        def _(k=k):
            lands[k][...] = jnp.zeros(lands[k].shape, lands[k].dtype)
    exchange(sends, lands, send_sem, recv_sem)()
    corner = {(0, 0): 0, (0, by - 1): 1, (bx - 1, 0): 2, (bx - 1, by - 1): 3}
    for x in range(bx):
        for y in range(by):
            total = loc_ref[x, y]
            for at, edge, k in ((x, 0, 0), (x, bx - 1, 1)):
                if at == edge:
                    total = total + rx[k, y].astype(jnp.float32)
            for at, edge, k in ((y, 0, 0), (y, by - 1, 1)):
                if at == edge:
                    total = total + ry[k, x].astype(jnp.float32)
            for place, k in (((0, 0), 0), ((0, by - 1), 1), ((bx - 1, 0), 2), ((bx - 1, by - 1), 3)):
                if (x, y) == place:
                    total = total + rc[k].astype(jnp.float32)
            out_ref[x, y] = total.astype(out_ref.dtype)


def local(coeffs, permit, shift_diag, codes, counts, weights, vectors):
    bx, by, coupling, order = coeffs.shape
    nv = vectors.shape[3]
    bf16, f32 = jnp.bfloat16, jnp.float32
    anyspace = pl.BlockSpec(memory_space=pl.ANY)
    vmem = pl.BlockSpec(memory_space=pltpu.VMEM)
    smem = pl.BlockSpec(memory_space=pltpu.SMEM)
    halo = pl.pallas_call(
        halo_kernel,
        out_shape=(
            jax.ShapeDtypeStruct((2, by, coupling, order), bf16),
            jax.ShapeDtypeStruct((2, bx, coupling, order), bf16),
            jax.ShapeDtypeStruct((4, coupling, order), bf16),
        ),
        in_specs=[anyspace],
        out_specs=(anyspace,) * 3,
        scratch_shapes=[pltpu.SemaphoreType.DMA((8,)), pltpu.SemaphoreType.DMA((8,))],
        compiler_params=pltpu.CompilerParams(collective_id=0, has_side_effects=True),
        name="halo",
    )(coeffs)
    padded = (bx + 2) * (by + 2)
    fac, loc, px, py, pc = pl.pallas_call(
        factor_kernel,
        out_shape=(
            jax.ShapeDtypeStruct((bx, by, order, order), bf16),
            jax.ShapeDtypeStruct((bx, by, order, nv), f32),
            jax.ShapeDtypeStruct((2, by, order, nv), bf16),
            jax.ShapeDtypeStruct((2, bx, order, nv), bf16),
            jax.ShapeDtypeStruct((4, order, nv), bf16),
        ),
        in_specs=[anyspace] * 4 + [vmem, vmem, smem, smem, smem, vmem],
        out_specs=(vmem,) * 5,
        scratch_shapes=[
            pltpu.VMEM((padded, coupling, order), bf16),
            pltpu.VMEM((padded, order, coupling), bf16),
            pltpu.VMEM((bx * by, order, order), f32),
            pltpu.VMEM((padded, order, nv), f32),
            pltpu.SemaphoreType.DMA((3 * bx + 6,)),
        ],
        name="factor",
    )(coeffs, *halo, permit, shift_diag, codes, counts, weights, vectors)
    applied = pl.pallas_call(
        sum_kernel,
        out_shape=jax.ShapeDtypeStruct((bx, by, order, nv), bf16),
        in_specs=[vmem, anyspace, anyspace, anyspace],
        out_specs=vmem,
        scratch_shapes=[
            pltpu.VMEM((2, by, order, nv), bf16),
            pltpu.VMEM((2, bx, order, nv), bf16),
            pltpu.VMEM((4, order, nv), bf16),
            pltpu.SemaphoreType.DMA((8,)), pltpu.SemaphoreType.DMA((8,)),
        ],
        compiler_params=pltpu.CompilerParams(collective_id=1, has_side_effects=True),
        name="sums",
    )(loc, px, py, pc)
    return fac, applied


def solution(mesh):
    placed = (
        P("gx", "gy", None, None),
        P("gx", "gy", None),
        P("gx", "gy", None),
        P("gx", "gy", None),
        P("gx", "gy"),
        P("gx", "gy", None),
        P("gx", "gy", None, None),
    )
    return jax.shard_map(
        local,
        mesh=mesh,
        in_specs=placed,
        out_specs=(P("gx", "gy", None, None), P("gx", "gy", None, None)),
        check_vma=False,
    )
```

time: 472 us -> 248 us (0.53)
  other arithmetic: 374 us -> 0 us
  Pallas kernels: 0 us -> 243 us
  starting transfers between devices: 32.5 us -> 0 us
  local copies, waits for them, and re-layouts: 36.3 us -> 3.94 us
  waiting for transfers between devices: 21.4 us -> 0 us
  matrix products: 6.06 us -> 0 us
    another operation x7 -> x0, other arithmetic: 347 us -> none  [the longest x4 189 us: local(): cholesky_factor = jnp.linalg.cholesky(system)]
    pallas_call x0 -> x3, Pallas kernels: none -> 243 us  [the longest x1 209 us: local(): pl.pallas_call(factor_kernel, out_shape=(jax.ShapeDtypeStruct((bx, by, or...]
    ppermute x12 -> x0, starting transfers between devices: 32.5 us -> none  [the longest x6 17.5 us: extended(): lax.ppermute(lax.slice_in_dim(block, block.shape[dim] - width, None, axis...]
    ppermute x12 -> x0, waiting for transfers between devices: 21.4 us -> none  [the longest x6 11.9 us: extended(): lax.ppermute(lax.slice_in_dim(block, block.shape[dim] - width, None, axis...]
    select_n x6 -> x0, other arithmetic: 14.4 us -> none  [local(): jnp.take(flattened, flat_index.reshape(-1), axis=0)]
    select_n x6 -> x0, local copies, waits for them, and re-layouts: 13.7 us -> none  [local(): jnp.take(flattened, flat_index.reshape(-1), axis=0)]
    gather x6 -> x0, local copies, waits for them, and re-layouts: 10.8 us -> none  [local(): jnp.take(flattened, flat_index.reshape(-1), axis=0)]
  transfers between devices with their start and end apart: 12 -> 0, of which waited for: 7 -> 0; matrix products, arithmetic and copies ran while one was open for 2% -> 0% of each run, Pallas kernels for 0% -> 0%
where the time goes in v1:
time: 248 us; the launch traced here: 247 us
  Pallas kernels  243 us (98%)
  local copies, waits for them, and re-layouts  3.94 us (2%)
    pallas_call x1, Pallas kernels, local(): pl.pallas_call(factor_kernel, out_shape=(jax.ShapeDtypeStruct((bx, by, or...  209 us
    pallas_call x1, Pallas kernels, local(): pl.pallas_call(halo_kernel, out_shape=(jax.ShapeDtypeStruct((2, by, coupl...  19.5 us
    pallas_call x1, Pallas kernels, local(): pl.pallas_call(sum_kernel, out_shape=jax.ShapeDtypeStruct((bx, by, order,...  14.1 us

profile of v1, /device:TPU:4, one launch (start us, length us, event | category | flops | bytes accessed | tf_op | source)
XLA Modules:
  0.0 247.1 jit_solution(8793137314539196352)
XLA Ops:
  0.6 0.0 copy-start
  0.6 1.4 copy.9.codes_ref
  2.0 0.0 copy-done
  2.0 0.7 copy.10.weights_ref
  2.7 19.5 %halo.1 = (bf16[2,8,256,128]{3,2,1,0:T(8,128)(2,1)}, bf16[2,2,256,128]{3,2,1,0:T(8,128)(2,1)}, bf16[4,256,128]{2,1,0:T(8,128)(2,1)}) custom-call(bf16[2,8,256,128]{3,2,1,0:T(8,128)(2,1)} %c_ref.3), custom_call_target="tpu_custom_call" | custom-call | tf_op jit(solution)/shard_map/halo/pallas_call | solution.py:214
  22.2 209.0 %factor.1 = (bf16[2,8,128,128]{3,2,1,0:T(8,128)(2,1)}, f32[2,8,128,128]{3,2,1,0:T(8,128)}, bf16[2,8,128,128]{3,2,1,0:T(8,128)(2,1)}, bf16[2,2,128,128]{3,2,1,0:T(8,128)(2,1)}, bf16[4,128,128]{2,1,0:T(8,128)(2,1)}) custom-call(bf16[2,8,256,128]{3,2,1,0:T(8,128)(2,1)} %c_ref.3, bf16[2,8,256,128]{3,2,1,0:T(8,128)(2,1)} %get-tuple-element.10.hx_ref, ...), custom_call_target="tpu_custom_call" | custom-call | tf_op jit(solution)/shard_map/factor/pallas_call | solution.py:228
  231.2 14.1 %sums.1 = bf16[2,8,128,128]{3,2,1,0:T(8,128)(2,1)} custom-call(f32[2,8,128,128]{3,2,1,0:T(8,128)} %get-tuple-element.14.loc_ref, bf16[2,8,128,128]{3,2,1,0:T(8,128)(2,1)} %get-tuple-element.15.px_ref, bf16[2,2,128,128]{3,2,1,0:T(8,128)(2,1)} %get-tuple-element.16.py_ref, bf16[4,128,128]{2,1,0:T(8,128)(2,1)} %get-tuple-element.17.pc_ref), custom_call_target="tpu_custom_call" | custom-call | tf_op jit(solution)/shard_map/sums/pallas_call | solution.py:248
  245.3 1.9 copy.12
Async XLA Ops:
  0.6 1.4 copy-start

commit v2 on v1

--- a/solution.py
+++ b/solution.py
@@ -8,6 +8,7 @@
 from jax.sharding import PartitionSpec as P
 
 MESH = pl.DeviceIdType.MESH
+BASE = 32
 DIRS = ((1, 0), (-1, 0), (0, 1), (0, -1), (1, 1), (1, -1), (-1, 1), (-1, -1))
 
 
@@ -130,33 +131,68 @@
             acc = acc + jnp.dot(scaled, cs[n], preferred_element_type=jnp.float32)
         gs[i] = 0.5 * (acc + acc.T) + jnp.where(rows == lanes, shift_ref[x, pl.ds(y, 1), :], 0.0)
 
-    parts = 4
-    step = order // parts
-    for part in range(parts):
-        low = part * step
-        height = order - low
-        row_here = lax.broadcasted_iota(jnp.int32, (height, order), 0) + low
-        lane_row = lax.broadcasted_iota(jnp.int32, (1, order), 1)
-
-        @pl.loop(low, low + step)
-        def _(k):
-            below = row_here > k
-            pick = jnp.full((height, order), k, jnp.int32)
-            for b in range(blocks):
-                m = gs[b, low:, :]
-                r = gs[b, pl.ds(k, 1), :]
-                d = jnp.sum(jnp.where(lane_row == k, r, 0.0), axis=1, keepdims=True)
-                r = (r + jnp.where(lane_row == k, 1.0, 0.0)) / d
-                f = jnp.where(below, jnp.take_along_axis(m, pick, axis=1), 0.0)
-                gs[b, low:, :] = m - f * r
+    per = order // BASE
+    seg = lax.broadcasted_iota(jnp.int32, (BASE, order), 1) // BASE
+    place = lax.broadcasted_iota(jnp.int32, (BASE, order), 1) % BASE
+    row = lax.broadcasted_iota(jnp.int32, (BASE, order), 0)
+    for stage in range(per):
+        low = stage * BASE
+        high = low + BASE
+        packs = []
+        for g in range(blocks // per):
+            pack = None
+            for q in range(per):
+                piece = gs[g * per + q, low:high, :]
+                shift = (q * BASE - low) % order
+                piece = pltpu.roll(piece, shift, axis=1) if shift else piece
+                pack = piece if pack is None else jnp.where(seg == q, piece, pack)
+            packs.append(pack)
+        done = [[] for _ in packs]
+        scale = [[] for _ in packs]
+        for k in range(BASE):
+            top = k // 8 * 8
+            for g, m in enumerate(packs):
+                f = jnp.take_along_axis(m, seg[top:] * BASE + k, axis=1)
+                d = f[k - top:k - top + 1]
+                r = m[k - top:k - top + 1]
+                scale[g].append(lax.rsqrt(d))
+                r = (r + jnp.where(place[:1] == k, 1.0, 0.0)) * (1.0 / d)
+                m = m - jnp.where(row[top:] > k, f, 0.0) * r
+                if k % 8 == 7:
+                    done[g].append(m[:8])
+                    m = m[8:]
+                packs[g] = m
+        for g in range(len(packs)):
+            m = jnp.concatenate(done[g], axis=0)
+            unit = jnp.where(row > place, m, jnp.where(row == place, 1.0, 0.0))
+            inv = unit * jnp.concatenate(scale[g], axis=0)
+            wide_inv = jnp.concatenate([jnp.where(seg == q, inv, 0.0) for q in range(per)], axis=0)
+            panel = []
+            for q in range(per):
+                here = gs[g * per + q, low:high, :]
+                panel.append(jnp.where(seg == stage, jnp.where(row == place, 1.0, 0.0), here))
+            panel = jnp.concatenate(panel, axis=0)
+            whole = jnp.dot(wide_inv, panel, precision=lax.Precision.HIGHEST, preferred_element_type=jnp.float32)
+            for q in range(per):
+                at = g * per + q
+                part = whole[q * BASE:(q + 1) * BASE]
+                gs[at, low:high, :] = jnp.where(seg <= stage, part, 0.0)
+                if high < order:
+                    h = part.astype(jnp.bfloat16)
+                    rest = part - h.astype(jnp.float32)
+                    m = rest.astype(jnp.bfloat16)
+                    l = (rest - m.astype(jnp.float32)).astype(jnp.bfloat16)
+                    update = lax.dot_general(
+                        jnp.concatenate([h, h, m, h, l, m], axis=0), jnp.concatenate([h, m, h, l, h, m], axis=0),
+                        (((0,), (0,)), ((), ())), preferred_element_type=jnp.float32)
+                    below = gs[at, high:, :]
+                    below = jnp.where(lanes[high:] // BASE == stage, 0.0, below)
+                    gs[at, high:, :] = below - update[high:]
 
     @pl.loop(0, blocks)
     def _(i):
         x, y = i // by, i % by
-        m = gs[i]
-        d = jnp.sum(jnp.where(rows == lanes, m, 0.0), axis=1, keepdims=True)
-        inverse = jnp.where(rows > lanes, m, jnp.where(rows == lanes, 1.0, 0.0)) * lax.rsqrt(d)
-        factor = inverse.astype(jnp.bfloat16)
+        factor = gs[i].astype(jnp.bfloat16)
         fac_ref[x, y] = factor
         image = lax.dot_general(factor, v_ref[x, y], (((0,), (0,)), ((), ())), preferred_element_type=jnp.float32)
         for s in range(slots):

time: 248 us -> 72.1 us (0.29)
  Pallas kernels: 243 us -> 66.3 us
    pallas_call x1, Pallas kernels: 209 us -> 32.7 us  [local(): pl.pallas_call(factor_kernel, out_shape=(jax.ShapeDtypeStruct((bx, by, or...]
where the time goes in v2:
time: 72.1 us; the launch traced here: 70.9 us
  Pallas kernels  66.3 us (92%)
  local copies, waits for them, and re-layouts  3.94 us (5%)
    pallas_call x1, Pallas kernels, local(): pl.pallas_call(factor_kernel, out_shape=(jax.ShapeDtypeStruct((bx, by, or...  32.7 us
    pallas_call x1, Pallas kernels, local(): pl.pallas_call(halo_kernel, out_shape=(jax.ShapeDtypeStruct((2, by, coupl...  19.5 us
    pallas_call x1, Pallas kernels, local(): pl.pallas_call(sum_kernel, out_shape=jax.ShapeDtypeStruct((bx, by, order,...  14.1 us
    unnamed x5, local copies, waits for them, and re-layouts  3.94 us

profile of v2, /device:TPU:4, one launch (start us, length us, event | category | flops | bytes accessed | tf_op | source)
XLA Modules:
  0.0 70.9 jit_solution(8624820060824620559)
XLA Ops:
  0.6 0.0 copy-start
  0.6 1.4 %copy.9.codes_ref = s32[2,8,6]{2,1,0:T(8,128)} copy(s32[2,8,6]{1,0,2:T(2,128)} %param.10) | data formatting | bytes 768 | tf_op args[3]
  2.0 0.0 copy-done
  2.0 0.7 copy.10.weights_ref
  2.7 19.5 %halo.1 = (bf16[2,8,256,128]{3,2,1,0:T(8,128)(2,1)}, bf16[2,2,256,128]{3,2,1,0:T(8,128)(2,1)}, bf16[4,256,128]{2,1,0:T(8,128)(2,1)}) custom-call(bf16[2,8,256,128]{3,2,1,0:T(8,128)(2,1)} %c_ref.3), custom_call_target="tpu_custom_call" | custom-call | tf_op jit(solution)/shard_map/halo/pallas_call | solution.py:250
  22.2 32.7 %factor.1 = (bf16[2,8,128,128]{3,2,1,0:T(8,128)(2,1)}, f32[2,8,128,128]{3,2,1,0:T(8,128)}, bf16[2,8,128,128]{3,2,1,0:T(8,128)(2,1)}, bf16[2,2,128,128]{3,2,1,0:T(8,128)(2,1)}, bf16[4,128,128]{2,1,0:T(8,128)(2,1)}) custom-call(bf16[2,8,256,128]{3,2,1,0:T(8,128)(2,1)} %c_ref.3, bf16[2,8,256,128]{3,2,1,0:T(8,128)(2,1)} %get-tuple-element.10.hx_ref, ...), custom_call_target="tpu_custom_call" | custom-call | tf_op jit(solution)/shard_map/factor/pallas_call | solution.py:264
  55.0 14.1 %sums.1 = bf16[2,8,128,128]{3,2,1,0:T(8,128)(2,1)} custom-call(f32[2,8,128,128]{3,2,1,0:T(8,128)} %get-tuple-element.14.loc_ref, bf16[2,8,128,128]{3,2,1,0:T(8,128)(2,1)} %get-tuple-element.15.px_ref, bf16[2,2,128,128]{3,2,1,0:T(8,128)(2,1)} %get-tuple-element.16.py_ref, bf16[4,128,128]{2,1,0:T(8,128)(2,1)} %get-tuple-element.17.pc_ref), custom_call_target="tpu_custom_call" | custom-call | tf_op jit(solution)/shard_map/sums/pallas_call | solution.py:284
  69.1 1.9 %copy.12 = bf16[2,8,128,128]{3,2,1,0:T(8,128)(2,1)} copy(bf16[2,8,128,128]{3,2,1,0:T(8,128)(2,1)} %sums.1) | data formatting | bytes 1048576
Async XLA Ops:
  0.6 1.4 %copy-start = (f32[2,8,6]{1,0,2:T(2,128)S(1)}, f32[2,8,6]{1,0,2:T(2,128)}, u32[]{:S(2)}) copy-start(f32[2,8,6]{1,0,2:T(2,128)} %param.12) | copy-start | bytes 1156

commit v3 on v2

--- a/solution.py
+++ b/solution.py
@@ -64,73 +64,195 @@
     return finish
 
 
-def halo_kernel(c_ref, hx_ref, hy_ref, hc_ref, send_sem, recv_sem):
-    bx, by = c_ref.shape[0], c_ref.shape[1]
+def gram_kernel(c_ref, permit_ref, shift_ref, codes_ref, counts_ref, gram_ref, cs, ts, own_sem, send_sem, recv_sem):
+    bx, by, coupling, order = c_ref.shape
+    slots = codes_ref.shape[0]
+    wide = by + 2
+    there, exists = neighbours()
     row = {1: bx - 1, -1: 0}
     col = {1: by - 1, -1: 0}
-    sends = [c_ref.at[bx - 1], c_ref.at[0], c_ref.at[:, by - 1], c_ref.at[:, 0]]
-    lands = [hx_ref.at[0], hx_ref.at[1], hy_ref.at[0], hy_ref.at[1]]
-    for k, d in enumerate(DIRS[4:]):
-        sends.append(c_ref.at[row[d[0]], col[d[1]]])
-        lands.append(hc_ref.at[k])
-    exchange(sends, lands, send_sem, recv_sem)()
-
-
-def factor_kernel(c_ref, hx_ref, hy_ref, hc_ref, permit_ref, shift_ref, codes_ref, counts_ref, weights_ref,
-                  v_ref, fac_ref, loc_ref, px_ref, py_ref, pc_ref, cs, ts, gs, ss, sem):
-    bx, by, coupling, order = c_ref.shape
-    slots = codes_ref.shape[2]
+    land_row = {1: 0, -1: bx + 1}
+    land_col = {1: 0, -1: by + 1}
+    gx_dirs, gy_dirs, corners = DIRS[:2], DIRS[2:4], DIRS[4:]
+    own = [pltpu.make_async_copy(c_ref.at[x], cs.at[pl.ds((x + 1) * wide + 1, by)], own_sem.at[x]) for x in range(bx)]
+    for copy in own:
+        copy.start()
+    barrier = pltpu.get_barrier_semaphore()
+    for d in DIRS:
+        @pl.when(exists(d))
+        def _(d=d):
+            pl.semaphore_signal(barrier, inc=1, device_id=there(d), device_id_type=MESH)
+    near = [exists(d).astype(jnp.int32) for d in DIRS[:4]]
+    pl.semaphore_wait(barrier, (near[0] + near[1] + 1) * (near[2] + near[3] + 1) - 1)
+
+    def remote(source, target, k, d):
+        return pltpu.make_async_remote_copy(
+            src_ref=source, dst_ref=cs.at[target], send_sem=send_sem.at[k], recv_sem=recv_sem.at[k],
+            device_id=there(d), device_id_type=MESH)
+
+    def gy_copy(j, x):
+        d = gy_dirs[j]
+        return remote(c_ref.at[x, col[d[1]]], (x + 1) * wide + land_col[d[1]], 4 + j * bx + x, d)
+
+    def corner_copy(j):
+        d = corners[j]
+        return remote(c_ref.at[row[d[0]], col[d[1]]], land_row[d[0]] * wide + land_col[d[1]], j, d)
+
+    def gx_copy(j, y):
+        d = gx_dirs[j]
+        return remote(c_ref.at[row[d[0]], y], land_row[d[0]] * wide + y + 1, 4 + 2 * bx + 2 * y + j, d)
+
+    for j, d in enumerate(corners):
+        @pl.when(exists(d))
+        def _(j=j):
+            corner_copy(j).start()
+    for j, d in enumerate(gx_dirs):
+        @pl.when(exists(d))
+        def _(j=j):
+            for y in range(by):
+                gx_copy(j, y).start()
+    for j, d in enumerate(gy_dirs):
+        @pl.when(exists(d))
+        def _(j=j):
+            for x in range(bx):
+                gy_copy(j, x).start()
+
+    zero = jnp.zeros((coupling, order), cs.dtype)
+    for j, d in enumerate(corners):
+        @pl.when(jnp.logical_not(exists((-d[0], -d[1]))))
+        def _(d=d):
+            cs[land_row[d[0]] * wide + land_col[d[1]]] = zero
+    for j, d in enumerate(gx_dirs):
+        @pl.when(jnp.logical_not(exists((-d[0], -d[1]))))
+        def _(d=d):
+            @pl.loop(0, by)
+            def _(y):
+                cs[land_row[d[0]] * wide + y + 1] = zero
+    for j, d in enumerate(gy_dirs):
+        @pl.when(jnp.logical_not(exists((-d[0], -d[1]))))
+        def _(d=d):
+            for x in range(bx):
+                cs[(x + 1) * wide + land_col[d[1]]] = zero
+
+    def turn(n):
+        ts[n] = cs[n].T
+
+    def terms(x, y, pairs):
+        p = permit_ref[x, pl.ds(y, 1), :]
+        acc = None
+        for ax, ay in pairs:
+            n = (x + ax) * wide + y + ay
+            times = jnp.int32(0)
+            for s in range(slots):
+                hit = (codes_ref[s, x, y] == ax * 3 + ay) & (s < counts_ref[x, y])
+                times = times + hit.astype(jnp.int32)
+            scaled = (ts[n].astype(jnp.float32) * p).astype(jnp.bfloat16)
+            term = times.astype(jnp.float32) * jnp.dot(scaled, cs[n], preferred_element_type=jnp.float32)
+            acc = term if acc is None else acc + term
+        return acc
+
+    inside = {x: [ax for ax in range(3) if 0 <= x + ax - 1 < bx] for x in range(bx)}
+    outside = {x: [ax for ax in range(3) if not 0 <= x + ax - 1 < bx] for x in range(bx)}
+    for copy in own:
+        copy.wait()
+    for x in range(bx):
+        @pl.loop(0, by)
+        def _(y):
+            turn((x + 1) * wide + y + 1)
+    for x in range(bx):
+        @pl.loop(1, by - 1)
+        def _(y):
+            gram_ref[x, y] = terms(x, y, [(ax, ay) for ax in inside[x] for ay in range(3)])
+    for j, d in enumerate(gy_dirs):
+        @pl.when(exists((-d[0], -d[1])))
+        def _(j=j):
+            for x in range(bx):
+                gy_copy(j, x).wait_recv()
+    for x in range(bx):
+        turn((x + 1) * wide)
+        turn((x + 1) * wide + by + 1)
+    for x in range(bx):
+        @pl.loop(0, 2)
+        def _(e):
+            y = e * (by - 1)
+            gram_ref[x, y] = terms(x, y, [(ax, ay) for ax in inside[x] for ay in range(3)])
+
+    same = lax.broadcasted_iota(jnp.int32, (order, order), 0) == lax.broadcasted_iota(jnp.int32, (order, order), 1)
+
+    def finished(x, y, acc):
+        gram_ref[x, y] = 0.5 * (acc + acc.T) + jnp.where(same, shift_ref[x, pl.ds(y, 1), :], 0.0)
+
+    for x in range(1, bx - 1):
+        @pl.loop(0, by)
+        def _(y):
+            finished(x, y, gram_ref[x, y])
+    for j, d in enumerate(corners):
+        @pl.when(exists((-d[0], -d[1])))
+        def _(j=j):
+            corner_copy(j).wait_recv()
+    for r in (0, bx + 1):
+        turn(r * wide)
+        turn(r * wide + by + 1)
+
+    def arrive(y):
+        for j, d in enumerate(gx_dirs):
+            @pl.when(exists((-d[0], -d[1])))
+            def _(j=j):
+                gx_copy(j, y).wait_recv()
+        turn(y + 1)
+        turn((bx + 1) * wide + y + 1)
+
+    def last(y):
+        for x in sorted({0, bx - 1}):
+            finished(x, y, gram_ref[x, y] + terms(x, y, [(ax, ay) for ax in outside[x] for ay in range(3)]))
+
+    arrive(0)
+
+    @pl.loop(1, by)
+    def _(y):
+        arrive(y)
+        last(y - 1)
+
+    last(by - 1)
+    for j, d in enumerate(corners):
+        @pl.when(exists(d))
+        def _(j=j):
+            corner_copy(j).wait_send()
+    for j, d in enumerate(gx_dirs):
+        @pl.when(exists(d))
+        def _(j=j):
+            for y in range(by):
+                gx_copy(j, y).wait_send()
+    for j, d in enumerate(gy_dirs):
+        @pl.when(exists(d))
+        def _(j=j):
+            for x in range(bx):
+                gy_copy(j, x).wait_send()
+
+
+def factor_kernel(gram_ref, codes_ref, counts_ref, weights_ref, v_ref, fac_ref, loc_ref, px_ref, py_ref, pc_ref, gs, ss):
+    bx, by, order = gram_ref.shape[:3]
+    slots = codes_ref.shape[0]
     blocks = bx * by
     wide = by + 2
     nx, ny = lax.axis_size("gx"), lax.axis_size("gy")
     gx, gy = lax.axis_index("gx"), lax.axis_index("gy")
-    moves = []
-    for x in range(bx):
-        moves.append((c_ref.at[x], cs.at[pl.ds((x + 1) * wide + 1, by)]))
-        moves.append((hy_ref.at[0, x], cs.at[(x + 1) * wide]))
-        moves.append((hy_ref.at[1, x], cs.at[(x + 1) * wide + by + 1]))
-    moves.append((hx_ref.at[0], cs.at[pl.ds(1, by)]))
-    moves.append((hx_ref.at[1], cs.at[pl.ds((bx + 1) * wide + 1, by)]))
-    moves.append((hc_ref.at[0], cs.at[0]))
-    moves.append((hc_ref.at[1], cs.at[by + 1]))
-    moves.append((hc_ref.at[2], cs.at[(bx + 1) * wide]))
-    moves.append((hc_ref.at[3], cs.at[(bx + 1) * wide + by + 1]))
-    copies = [pltpu.make_async_copy(a, b, sem.at[k]) for k, (a, b) in enumerate(moves)]
-    for copy in copies:
-        copy.start()
 
     @pl.loop(0, (bx + 2) * wide)
     def _(n):
         ss[n] = jnp.zeros(ss.shape[1:], ss.dtype)
 
-    for copy in copies:
-        copy.wait()
-
-    @pl.loop(0, (bx + 2) * wide)
-    def _(n):
-        ts[n] = cs[n].T
+    for i in range(blocks):
+        gs[i] = gram_ref[i // by, i % by]
 
     def slot_at(x, y, s):
-        code = codes_ref[x, y, s]
+        code = codes_ref[s, x, y]
         ax, ay = code // 3, code % 3
         whole_x, whole_y = gx * bx + x + ax - 1, gy * by + y + ay - 1
         ok = (s < counts_ref[x, y]) & (whole_x >= 0) & (whole_x < nx * bx) & (whole_y >= 0) & (whole_y < ny * by)
         return jnp.where(ok, (x + ax) * wide + y + ay, (x + 1) * wide + y + 1), ok
 
-    rows = lax.broadcasted_iota(jnp.int32, (order, order), 0)
     lanes = lax.broadcasted_iota(jnp.int32, (order, order), 1)
-
-    @pl.loop(0, blocks)
-    def _(i):
-        x, y = i // by, i % by
-        p = permit_ref[x, pl.ds(y, 1), :]
-        acc = jnp.zeros((order, order), jnp.float32)
-        for s in range(slots):
-            n, ok = slot_at(x, y, s)
-            scaled = (ts[n].astype(jnp.float32) * jnp.where(ok, p, 0.0)).astype(jnp.bfloat16)
-            acc = acc + jnp.dot(scaled, cs[n], preferred_element_type=jnp.float32)
-        gs[i] = 0.5 * (acc + acc.T) + jnp.where(rows == lanes, shift_ref[x, pl.ds(y, 1), :], 0.0)
-
     per = order // BASE
     seg = lax.broadcasted_iota(jnp.int32, (BASE, order), 1) // BASE
     place = lax.broadcasted_iota(jnp.int32, (BASE, order), 1) % BASE
@@ -197,7 +319,7 @@
         image = lax.dot_general(factor, v_ref[x, y], (((0,), (0,)), ((), ())), preferred_element_type=jnp.float32)
         for s in range(slots):
             n, ok = slot_at(x, y, s)
-            w = jnp.where(ok, weights_ref[x, y, s], 0.0)
+            w = jnp.where(ok, weights_ref[s, x, y], 0.0)
             ss[n] = ss[n] + w * image
 
     for x in range(bx):
@@ -247,20 +369,23 @@
     anyspace = pl.BlockSpec(memory_space=pl.ANY)
     vmem = pl.BlockSpec(memory_space=pltpu.VMEM)
     smem = pl.BlockSpec(memory_space=pltpu.SMEM)
-    halo = pl.pallas_call(
-        halo_kernel,
-        out_shape=(
-            jax.ShapeDtypeStruct((2, by, coupling, order), bf16),
-            jax.ShapeDtypeStruct((2, bx, coupling, order), bf16),
-            jax.ShapeDtypeStruct((4, coupling, order), bf16),
-        ),
-        in_specs=[anyspace],
-        out_specs=(anyspace,) * 3,
-        scratch_shapes=[pltpu.SemaphoreType.DMA((8,)), pltpu.SemaphoreType.DMA((8,))],
+    codes, weights = jnp.transpose(codes, (2, 0, 1)), jnp.transpose(weights, (2, 0, 1))
+    padded = (bx + 2) * (by + 2)
+    copies = 4 + 2 * bx + 2 * by
+    gram = pl.pallas_call(
+        gram_kernel,
+        out_shape=jax.ShapeDtypeStruct((bx, by, order, order), f32),
+        in_specs=[anyspace, vmem, vmem, smem, smem],
+        out_specs=vmem,
+        scratch_shapes=[
+            pltpu.VMEM((padded, coupling, order), bf16),
+            pltpu.VMEM((padded, order, coupling), bf16),
+            pltpu.SemaphoreType.DMA((bx,)),
+            pltpu.SemaphoreType.DMA((copies,)), pltpu.SemaphoreType.DMA((copies,)),
+        ],
         compiler_params=pltpu.CompilerParams(collective_id=0, has_side_effects=True),
-        name="halo",
-    )(coeffs)
-    padded = (bx + 2) * (by + 2)
+        name="gram",
+    )(coeffs, permit, shift_diag, codes, counts)
     fac, loc, px, py, pc = pl.pallas_call(
         factor_kernel,
         out_shape=(
@@ -270,17 +395,14 @@
             jax.ShapeDtypeStruct((2, bx, order, nv), bf16),
             jax.ShapeDtypeStruct((4, order, nv), bf16),
         ),
-        in_specs=[anyspace] * 4 + [vmem, vmem, smem, smem, smem, vmem],
+        in_specs=[vmem, smem, smem, smem, vmem],
         out_specs=(vmem,) * 5,
         scratch_shapes=[
-            pltpu.VMEM((padded, coupling, order), bf16),
-            pltpu.VMEM((padded, order, coupling), bf16),
             pltpu.VMEM((bx * by, order, order), f32),
             pltpu.VMEM((padded, order, nv), f32),
-            pltpu.SemaphoreType.DMA((3 * bx + 6,)),
         ],
         name="factor",
-    )(coeffs, *halo, permit, shift_diag, codes, counts, weights, vectors)
+    )(gram, codes, counts, weights, vectors)
     applied = pl.pallas_call(
         sum_kernel,
         out_shape=jax.ShapeDtypeStruct((bx, by, order, nv), bf16),

time: 72.1 us -> 61.8 us (0.86)
  Pallas kernels: 66.3 us -> 58.2 us
  local copies, waits for them, and re-layouts: 3.94 us -> 1.89 us
    pallas_call x1, Pallas kernels: 32.7 us -> 22.8 us  [local(): pl.pallas_call(factor_kernel, out_shape=(jax.ShapeDtypeStruct((bx, by, or...]
    pallas_call x1, Pallas kernels: 19.5 us -> 22.4 us  [local(): pl.pallas_call(gram_kernel, out_shape=jax.ShapeDtypeStruct((bx, by, order...]
    unnamed x5 -> x1, local copies, waits for them, and re-layouts: 3.94 us -> 1.89 us
    pallas_call x1, Pallas kernels: 14.1 us -> 13 us  [local(): pl.pallas_call(sum_kernel, out_shape=jax.ShapeDtypeStruct((bx, by, order,...]
where the time goes in v3:
time: 61.8 us; the launch traced here: 60.7 us
  Pallas kernels  58.2 us (94%)
  local copies, waits for them, and re-layouts  1.89 us (3%)
  between operations  0.65 us (1%)
    pallas_call x1, Pallas kernels, local(): pl.pallas_call(factor_kernel, out_shape=(jax.ShapeDtypeStruct((bx, by, or...  22.8 us
    pallas_call x1, Pallas kernels, local(): pl.pallas_call(gram_kernel, out_shape=jax.ShapeDtypeStruct((bx, by, order...  22.4 us
    pallas_call x1, Pallas kernels, local(): pl.pallas_call(sum_kernel, out_shape=jax.ShapeDtypeStruct((bx, by, order,...  13 us
    unnamed x1, local copies, waits for them, and re-layouts  1.89 us

profile of v3, /device:TPU:4, one launch (start us, length us, event | category | flops | bytes accessed | tf_op | source)
XLA Modules:
  0.0 60.7 jit_solution(18341704874461261590)
XLA Ops:
  0.6 22.4 %gram.1.gram_ref = f32[2,8,128,128]{3,2,1,0:T(8,128)} custom-call(bf16[2,8,256,128]{3,2,1,0:T(8,128)(2,1)} %c_ref.1, f32[2,8,256]{2,1,0:T(8,128)} %permit_ref.1, f32[2,8,128]{2,1,0:T(8,128)} %shift_ref.1, s32[6,2,8]{2,1,0:T(2,128)} %bitcast.2, s32[2,8]{1,0:T(2,128)} %counts_ref.3), custom_call_target="tpu_custom_call" | custom-call | tf_op jit(solution)/shard_map/gram/pallas_call | solution.py:375
  23.0 22.8 %factor.1 = (bf16[2,8,128,128]{3,2,1,0:T(8,128)(2,1)}, f32[2,8,128,128]{3,2,1,0:T(8,128)}, bf16[2,8,128,128]{3,2,1,0:T(8,128)(2,1)}, bf16[2,2,128,128]{3,2,1,0:T(8,128)(2,1)}, bf16[4,128,128]{2,1,0:T(8,128)(2,1)}) custom-call(f32[2,8,128,128]{3,2,1,0:T(8,128)} %gram.1.gram_ref, s32[6,2,8]{2,1,0:T(2,128)} %bitcast.3, s32[2,8]{1,0:T(2,128)} %counts_ref.3, ...), custom_call_target="tpu_custom_call" | custom-call | tf_op jit(solution)/shard_map/factor/pallas_call | solution.py:389
  45.8 13.0 %sums.1 = bf16[2,8,128,128]{3,2,1,0:T(8,128)(2,1)} custom-call(f32[2,8,128,128]{3,2,1,0:T(8,128)} %get-tuple-element.8.loc_ref, bf16[2,8,128,128]{3,2,1,0:T(8,128)(2,1)} %get-tuple-element.9.px_ref, bf16[2,2,128,128]{3,2,1,0:T(8,128)(2,1)} %get-tuple-element.10.py_ref, bf16[4,128,128]{2,1,0:T(8,128)(2,1)} %get-tuple-element.11.pc_ref), custom_call_target="tpu_custom_call" | custom-call | tf_op jit(solution)/shard_map/sums/pallas_call | solution.py:406
  58.8 1.9 %copy.10 = bf16[2,8,128,128]{3,2,1,0:T(8,128)(2,1)} copy(bf16[2,8,128,128]{3,2,1,0:T(8,128)(2,1)} %sums.1) | data formatting | bytes 1048576

commit v4 on v3

--- a/solution.py
+++ b/solution.py
@@ -271,16 +271,24 @@
             packs.append(pack)
         done = [[] for _ in packs]
         scale = [[] for _ in packs]
-        for k in range(BASE):
+        for k in range(0, BASE, 2):
             top = k // 8 * 8
+            at, nxt = k - top, k + 1 - top
             for g, m in enumerate(packs):
                 f = jnp.take_along_axis(m, seg[top:] * BASE + k, axis=1)
-                d = f[k - top:k - top + 1]
-                r = m[k - top:k - top + 1]
+                f_next = jnp.take_along_axis(m, seg[top:] * BASE + (k + 1), axis=1)
+                d = f[at:at + 1]
+                inv_d = 1.0 / d
                 scale[g].append(lax.rsqrt(d))
-                r = (r + jnp.where(place[:1] == k, 1.0, 0.0)) * (1.0 / d)
-                m = m - jnp.where(row[top:] > k, f, 0.0) * r
-                if k % 8 == 7:
+                f = jnp.where(row[top:] > k, f, 0.0)
+                f_next = f_next - f * (f_next[at:at + 1] * inv_d)
+                d_next = f_next[nxt:nxt + 1]
+                scale[g].append(lax.rsqrt(d_next))
+                m = m - f * ((m[at:at + 1] + jnp.where(place[:1] == k, 1.0, 0.0)) * inv_d)
+                f_next = jnp.where(row[top:] > k + 1, f_next, 0.0)
+                r_next = m[nxt:nxt + 1] + jnp.where(place[:1] == k + 1, 1.0, 0.0)
+                m = m - f_next * (r_next * (1.0 / d_next))
+                if k % 8 == 6:
                     done[g].append(m[:8])
                     m = m[8:]
                 packs[g] = m

time: 61.8 us -> 58.3 us (0.943)
  Pallas kernels: 58.2 us -> 54.6 us
    pallas_call x1, Pallas kernels: 22.8 us -> 19.3 us  [local(): pl.pallas_call(factor_kernel, out_shape=(jax.ShapeDtypeStruct((bx, by, or...]
where the time goes in v4:
time: 58.3 us; the launch traced here: 57.2 us
  Pallas kernels  54.6 us (94%)
  local copies, waits for them, and re-layouts  1.89 us (3%)
  between operations  0.65 us (1%)
    pallas_call x1, Pallas kernels, local(): pl.pallas_call(gram_kernel, out_shape=jax.ShapeDtypeStruct((bx, by, order...  22.4 us
    pallas_call x1, Pallas kernels, local(): pl.pallas_call(factor_kernel, out_shape=(jax.ShapeDtypeStruct((bx, by, or...  19.3 us
    pallas_call x1, Pallas kernels, local(): pl.pallas_call(sum_kernel, out_shape=jax.ShapeDtypeStruct((bx, by, order,...  13 us
    unnamed x1, local copies, waits for them, and re-layouts  1.89 us

profile of v4, /device:TPU:4, one launch (start us, length us, event | category | flops | bytes accessed | tf_op | source)
XLA Modules:
  0.0 57.2 jit_solution(1823197835897944695)
XLA Ops:
  0.6 22.4 %gram.1.gram_ref = f32[2,8,128,128]{3,2,1,0:T(8,128)} custom-call(bf16[2,8,256,128]{3,2,1,0:T(8,128)(2,1)} %c_ref.1, f32[2,8,256]{2,1,0:T(8,128)} %permit_ref.1, f32[2,8,128]{2,1,0:T(8,128)} %shift_ref.1, s32[6,2,8]{2,1,0:T(2,128)} %bitcast.2, s32[2,8]{1,0:T(2,128)} %counts_ref.3), custom_call_target="tpu_custom_call" | custom-call | tf_op jit(solution)/shard_map/gram/pallas_call | solution.py:383
  23.0 19.3 %factor.1 = (bf16[2,8,128,128]{3,2,1,0:T(8,128)(2,1)}, f32[2,8,128,128]{3,2,1,0:T(8,128)}, bf16[2,8,128,128]{3,2,1,0:T(8,128)(2,1)}, bf16[2,2,128,128]{3,2,1,0:T(8,128)(2,1)}, bf16[4,128,128]{2,1,0:T(8,128)(2,1)}) custom-call(f32[2,8,128,128]{3,2,1,0:T(8,128)} %gram.1.gram_ref, s32[6,2,8]{2,1,0:T(2,128)} %bitcast.3, s32[2,8]{1,0:T(2,128)} %counts_ref.3, ...), custom_call_target="tpu_custom_call" | custom-call | tf_op jit(solution)/shard_map/factor/pallas_call | solution.py:397
  42.3 13.0 %sums.1 = bf16[2,8,128,128]{3,2,1,0:T(8,128)(2,1)} custom-call(f32[2,8,128,128]{3,2,1,0:T(8,128)} %get-tuple-element.8.loc_ref, bf16[2,8,128,128]{3,2,1,0:T(8,128)(2,1)} %get-tuple-element.9.px_ref, bf16[2,2,128,128]{3,2,1,0:T(8,128)(2,1)} %get-tuple-element.10.py_ref, bf16[4,128,128]{2,1,0:T(8,128)(2,1)} %get-tuple-element.11.pc_ref), custom_call_target="tpu_custom_call" | custom-call | tf_op jit(solution)/shard_map/sums/pallas_call | solution.py:414
  55.3 1.9 %copy.10 = bf16[2,8,128,128]{3,2,1,0:T(8,128)(2,1)} copy(bf16[2,8,128,128]{3,2,1,0:T(8,128)(2,1)} %sums.1) | data formatting | bytes 1048576

commit v5 on v4

--- a/solution.py
+++ b/solution.py
@@ -29,39 +29,6 @@
         return ok
 
     return there, exists
-
-
-def exchange(sends, lands, send_sem, recv_sem, before=None):
-    there, exists = neighbours()
-    barrier = pltpu.get_barrier_semaphore()
-    for d in DIRS:
-        @pl.when(exists(d))
-        def _(d=d):
-            pl.semaphore_signal(barrier, inc=1, device_id=there(d), device_id_type=MESH)
-    near = [exists(d).astype(jnp.int32) for d in DIRS[:4]]
-    pl.semaphore_wait(barrier, (near[0] + near[1] + 1) * (near[2] + near[3] + 1) - 1)
-
-    def copy(k, d):
-        return pltpu.make_async_remote_copy(
-            src_ref=sends[k], dst_ref=lands[k], send_sem=send_sem.at[k], recv_sem=recv_sem.at[k],
-            device_id=there(d), device_id_type=MESH)
-
-    for k, d in enumerate(DIRS):
-        @pl.when(exists(d))
-        def _(k=k, d=d):
-            copy(k, d).start()
-
-    def finish():
-        for k, d in enumerate(DIRS):
-            @pl.when(exists((-d[0], -d[1])))
-            def _(k=k, d=d):
-                copy(k, d).wait_recv()
-        for k, d in enumerate(DIRS):
-            @pl.when(exists(d))
-            def _(k=k, d=d):
-                copy(k, d).wait_send()
-
-    return finish
 
 
 def gram_kernel(c_ref, permit_ref, shift_ref, codes_ref, counts_ref, gram_ref, cs, ts, own_sem, send_sem, recv_sem):
@@ -230,27 +197,11 @@
                 gy_copy(j, x).wait_send()
 
 
-def factor_kernel(gram_ref, codes_ref, counts_ref, weights_ref, v_ref, fac_ref, loc_ref, px_ref, py_ref, pc_ref, gs, ss):
+def factor_kernel(gram_ref, fac_ref, gs):
     bx, by, order = gram_ref.shape[:3]
-    slots = codes_ref.shape[0]
     blocks = bx * by
-    wide = by + 2
-    nx, ny = lax.axis_size("gx"), lax.axis_size("gy")
-    gx, gy = lax.axis_index("gx"), lax.axis_index("gy")
-
-    @pl.loop(0, (bx + 2) * wide)
-    def _(n):
-        ss[n] = jnp.zeros(ss.shape[1:], ss.dtype)
-
     for i in range(blocks):
         gs[i] = gram_ref[i // by, i % by]
-
-    def slot_at(x, y, s):
-        code = codes_ref[s, x, y]
-        ax, ay = code // 3, code % 3
-        whole_x, whole_y = gx * bx + x + ax - 1, gy * by + y + ay - 1
-        ok = (s < counts_ref[x, y]) & (whole_x >= 0) & (whole_x < nx * bx) & (whole_y >= 0) & (whole_y < ny * by)
-        return jnp.where(ok, (x + ax) * wide + y + ay, (x + 1) * wide + y + 1), ok
 
     lanes = lax.broadcasted_iota(jnp.int32, (order, order), 1)
     per = order // BASE
@@ -321,53 +272,93 @@
 
     @pl.loop(0, blocks)
     def _(i):
-        x, y = i // by, i % by
-        factor = gs[i].astype(jnp.bfloat16)
-        fac_ref[x, y] = factor
-        image = lax.dot_general(factor, v_ref[x, y], (((0,), (0,)), ((), ())), preferred_element_type=jnp.float32)
-        for s in range(slots):
-            n, ok = slot_at(x, y, s)
-            w = jnp.where(ok, weights_ref[s, x, y], 0.0)
-            ss[n] = ss[n] + w * image
-
-    for x in range(bx):
-        for y in range(by):
-            loc_ref[x, y] = ss[(x + 1) * wide + y + 1]
-        py_ref[1, x] = ss[(x + 1) * wide].astype(jnp.bfloat16)
-        py_ref[0, x] = ss[(x + 1) * wide + by + 1].astype(jnp.bfloat16)
-    for y in range(by):
-        px_ref[1, y] = ss[y + 1].astype(jnp.bfloat16)
-        px_ref[0, y] = ss[(bx + 1) * wide + y + 1].astype(jnp.bfloat16)
-    pc_ref[0] = ss[(bx + 1) * wide + by + 1].astype(jnp.bfloat16)
-    pc_ref[1] = ss[(bx + 1) * wide].astype(jnp.bfloat16)
-    pc_ref[2] = ss[by + 1].astype(jnp.bfloat16)
-    pc_ref[3] = ss[0].astype(jnp.bfloat16)
-
-
-def sum_kernel(loc_ref, px_ref, py_ref, pc_ref, out_ref, rx, ry, rc, send_sem, recv_sem):
-    bx, by = loc_ref.shape[0], loc_ref.shape[1]
-    _, exists = neighbours()
-    sends = [px_ref.at[0], px_ref.at[1], py_ref.at[0], py_ref.at[1]] + [pc_ref.at[k] for k in range(4)]
+        fac_ref[i // by, i % by] = gs[i].astype(fac_ref.dtype)
+
+
+def sum_kernel(fac_ref, v_ref, codes_ref, counts_ref, weights_ref, out_ref, img, loc, px, py, pc, rx, ry, rc, wt,
+               send_sem, recv_sem):
+    bx, by = fac_ref.shape[:2]
+    slots = codes_ref.shape[0]
+    there, exists = neighbours()
+    sends = [px.at[0], px.at[1], py.at[0], py.at[1]] + [pc.at[k] for k in range(4)]
     lands = [rx.at[0], rx.at[1], ry.at[0], ry.at[1]] + [rc.at[k] for k in range(4)]
+    barrier = pltpu.get_barrier_semaphore()
+    for d in DIRS:
+        @pl.when(exists(d))
+        def _(d=d):
+            pl.semaphore_signal(barrier, inc=1, device_id=there(d), device_id_type=MESH)
     for k, d in enumerate(DIRS):
         @pl.when(jnp.logical_not(exists((-d[0], -d[1]))))
         def _(k=k):
             lands[k][...] = jnp.zeros(lands[k].shape, lands[k].dtype)
-    exchange(sends, lands, send_sem, recv_sem)()
-    corner = {(0, 0): 0, (0, by - 1): 1, (bx - 1, 0): 2, (bx - 1, by - 1): 3}
+
+    @pl.loop(0, by)
+    def _(y):
+        for x in range(bx):
+            for offset in range(9):
+                w = jnp.float32(0.0)
+                for s in range(slots):
+                    hit = (codes_ref[s, x, y] == offset) & (s < counts_ref[x, y])
+                    w = w + jnp.where(hit, weights_ref[s, x, y], 0.0)
+                wt[offset, x * by + y] = w
+            img[x, y] = lax.dot_general(fac_ref[x, y], v_ref[x, y], (((0,), (0,)), ((), ())),
+                                        preferred_element_type=jnp.float32)
+
+    def target(tx, ty):
+        total = None
+        for x in range(bx):
+            for y in range(by):
+                ax, ay = tx - x, ty - y
+                if 0 <= ax < 3 and 0 <= ay < 3:
+                    term = wt[ax * 3 + ay, x * by + y] * img[x, y]
+                    total = term if total is None else total + term
+        return total
+
+    for y in range(by):
+        px[0, y] = target(bx + 1, y + 1).astype(px.dtype)
+        px[1, y] = target(0, y + 1).astype(px.dtype)
+    for k, d in enumerate(DIRS[4:]):
+        pc[k] = target(bx + 1 if d[0] > 0 else 0, by + 1 if d[1] > 0 else 0).astype(pc.dtype)
+    for x in range(bx):
+        py[0, x] = target(x + 1, by + 1).astype(py.dtype)
+        py[1, x] = target(x + 1, 0).astype(py.dtype)
+    near = [exists(d).astype(jnp.int32) for d in DIRS[:4]]
+    pl.semaphore_wait(barrier, (near[0] + near[1] + 1) * (near[2] + near[3] + 1) - 1)
+
+    def copy(k, d):
+        return pltpu.make_async_remote_copy(
+            src_ref=sends[k], dst_ref=lands[k], send_sem=send_sem.at[k], recv_sem=recv_sem.at[k],
+            device_id=there(d), device_id_type=MESH)
+
+    order_of = (4, 5, 6, 7, 0, 1, 2, 3)
+    for k in order_of:
+        @pl.when(exists(DIRS[k]))
+        def _(k=k):
+            copy(k, DIRS[k]).start()
     for x in range(bx):
         for y in range(by):
-            total = loc_ref[x, y]
-            for at, edge, k in ((x, 0, 0), (x, bx - 1, 1)):
-                if at == edge:
+            loc[x, y] = target(x + 1, y + 1)
+    for k in order_of:
+        @pl.when(exists((-DIRS[k][0], -DIRS[k][1])))
+        def _(k=k):
+            copy(k, DIRS[k]).wait_recv()
+    for x in range(bx):
+        for y in range(by):
+            total = loc[x, y]
+            for k, edge in ((0, 0), (1, bx - 1)):
+                if x == edge:
                     total = total + rx[k, y].astype(jnp.float32)
-            for at, edge, k in ((y, 0, 0), (y, by - 1, 1)):
-                if at == edge:
+            for k, edge in ((0, 0), (1, by - 1)):
+                if y == edge:
                     total = total + ry[k, x].astype(jnp.float32)
-            for place, k in (((0, 0), 0), ((0, by - 1), 1), ((bx - 1, 0), 2), ((bx - 1, by - 1), 3)):
+            for k, place in enumerate(((0, 0), (0, by - 1), (bx - 1, 0), (bx - 1, by - 1))):
                 if (x, y) == place:
                     total = total + rc[k].astype(jnp.float32)
             out_ref[x, y] = total.astype(out_ref.dtype)
+    for k in order_of:
+        @pl.when(exists(DIRS[k]))
+        def _(k=k):
+            copy(k, DIRS[k]).wait_send()
 
 
 def local(coeffs, permit, shift_diag, codes, counts, weights, vectors):
@@ -394,37 +385,34 @@
         compiler_params=pltpu.CompilerParams(collective_id=0, has_side_effects=True),
         name="gram",
     )(coeffs, permit, shift_diag, codes, counts)
-    fac, loc, px, py, pc = pl.pallas_call(
+    fac = pl.pallas_call(
         factor_kernel,
-        out_shape=(
-            jax.ShapeDtypeStruct((bx, by, order, order), bf16),
-            jax.ShapeDtypeStruct((bx, by, order, nv), f32),
-            jax.ShapeDtypeStruct((2, by, order, nv), bf16),
-            jax.ShapeDtypeStruct((2, bx, order, nv), bf16),
-            jax.ShapeDtypeStruct((4, order, nv), bf16),
-        ),
-        in_specs=[vmem, smem, smem, smem, vmem],
-        out_specs=(vmem,) * 5,
-        scratch_shapes=[
-            pltpu.VMEM((bx * by, order, order), f32),
-            pltpu.VMEM((padded, order, nv), f32),
-        ],
+        out_shape=jax.ShapeDtypeStruct((bx, by, order, order), bf16),
+        in_specs=[vmem],
+        out_specs=vmem,
+        scratch_shapes=[pltpu.VMEM((bx * by, order, order), f32)],
         name="factor",
-    )(gram, codes, counts, weights, vectors)
+    )(gram)
+    edges = [
+        pltpu.VMEM((2, by, order, nv), bf16),
+        pltpu.VMEM((2, bx, order, nv), bf16),
+        pltpu.VMEM((4, order, nv), bf16),
+    ]
     applied = pl.pallas_call(
         sum_kernel,
         out_shape=jax.ShapeDtypeStruct((bx, by, order, nv), bf16),
-        in_specs=[vmem, anyspace, anyspace, anyspace],
+        in_specs=[vmem, vmem, smem, smem, smem],
         out_specs=vmem,
         scratch_shapes=[
-            pltpu.VMEM((2, by, order, nv), bf16),
-            pltpu.VMEM((2, bx, order, nv), bf16),
-            pltpu.VMEM((4, order, nv), bf16),
+            pltpu.VMEM((bx, by, order, nv), f32),
+            pltpu.VMEM((bx, by, order, nv), f32),
+            *edges, *edges,
+            pltpu.SMEM((9, bx * by), f32),
             pltpu.SemaphoreType.DMA((8,)), pltpu.SemaphoreType.DMA((8,)),
         ],
         compiler_params=pltpu.CompilerParams(collective_id=1, has_side_effects=True),
         name="sums",
-    )(loc, px, py, pc)
+    )(fac, vectors, codes, counts, weights)
     return fac, applied
 
 

time: 58.3 us -> 55.1 us (0.945); the launches traced: 57.2 us -> 54.8 us
  Pallas kernels: 54.6 us -> 52.2 us
    pallas_call x1, Pallas kernels: 19.3 us -> 14.8 us  [local(): pl.pallas_call(factor_kernel, out_shape=jax.ShapeDtypeStruct((bx, by, ord...]
    pallas_call x1, Pallas kernels: 13 us -> 15.1 us  [local(): pl.pallas_call(sum_kernel, out_shape=jax.ShapeDtypeStruct((bx, by, order,...]
where the time goes in v5:
time: 55.1 us; the launch traced here: 54.8 us
  Pallas kernels  52.2 us (95%)
  local copies, waits for them, and re-layouts  1.89 us (3%)
  between operations  0.65 us (1%)
    pallas_call x1, Pallas kernels, local(): pl.pallas_call(gram_kernel, out_shape=jax.ShapeDtypeStruct((bx, by, order...  22.3 us
    pallas_call x1, Pallas kernels, local(): pl.pallas_call(sum_kernel, out_shape=jax.ShapeDtypeStruct((bx, by, order,...  15.1 us
    pallas_call x1, Pallas kernels, local(): pl.pallas_call(factor_kernel, out_shape=jax.ShapeDtypeStruct((bx, by, ord...  14.8 us
    unnamed x1, local copies, waits for them, and re-layouts  1.89 us

profile of v5, /device:TPU:4, one launch (start us, length us, event | category | flops | bytes accessed | tf_op | source)
XLA Modules:
  0.0 54.8 jit_solution(2794609313442395301)
XLA Ops:
  0.6 22.3 %gram.1.gram_ref = f32[2,8,128,128]{3,2,1,0:T(8,128)} custom-call(bf16[2,8,256,128]{3,2,1,0:T(8,128)(2,1)} %c_ref.1, f32[2,8,256]{2,1,0:T(8,128)} %permit_ref.1, f32[2,8,128]{2,1,0:T(8,128)} %shift_ref.1, s32[6,2,8]{2,1,0:T(2,128)} %bitcast.2, s32[2,8]{1,0:T(2,128)} %counts_ref.3), custom_call_target="tpu_custom_call" | custom-call | tf_op jit(solution)/shard_map/gram/pallas_call | solution.py:374
  23.0 14.8 %factor.1.fac_ref = bf16[2,8,128,128]{3,2,1,0:T(8,128)(2,1)} custom-call(f32[2,8,128,128]{3,2,1,0:T(8,128)} %gram.1.gram_ref), custom_call_target="tpu_custom_call" | custom-call | tf_op jit(solution)/shard_map/factor/pallas_call | solution.py:388
  37.8 15.1 %sums.1 = bf16[2,8,128,128]{3,2,1,0:T(8,128)(2,1)} custom-call(bf16[2,8,128,128]{3,2,1,0:T(8,128)(2,1)} %factor.1.fac_ref, bf16[2,8,128,128]{3,2,1,0:T(8,128)(2,1)} %v_ref.1, s32[6,2,8]{2,1,0:T(2,128)} %bitcast.3, s32[2,8]{1,0:T(2,128)} %counts_ref.3, f32[6,2,8]{2,1,0:T(2,128)} %bitcast.4), custom_call_target="tpu_custom_call" | custom-call | tf_op jit(solution)/shard_map/sums/pallas_call | solution.py:401
  52.9 1.9 %copy.10 = bf16[2,8,128,128]{3,2,1,0:T(8,128)(2,1)} copy(bf16[2,8,128,128]{3,2,1,0:T(8,128)(2,1)} %sums.1) | data formatting | bytes 1048576

commit v6 on v5

--- a/solution.py
+++ b/solution.py
@@ -31,7 +31,7 @@
     return there, exists
 
 
-def gram_kernel(c_ref, permit_ref, shift_ref, codes_ref, counts_ref, gram_ref, cs, ts, own_sem, send_sem, recv_sem):
+def gram_kernel(c_ref, permit_ref, shift_ref, codes_ref, counts_ref, weights_ref, gram_ref, wt, cs, ts, own_sem, send_sem, recv_sem):
     bx, by, coupling, order = c_ref.shape
     slots = codes_ref.shape[0]
     wide = by + 2
@@ -120,6 +120,17 @@
 
     inside = {x: [ax for ax in range(3) if 0 <= x + ax - 1 < bx] for x in range(bx)}
     outside = {x: [ax for ax in range(3) if not 0 <= x + ax - 1 < bx] for x in range(bx)}
+
+    @pl.loop(0, by)
+    def _(y):
+        for x in range(bx):
+            for offset in range(9):
+                w = jnp.float32(0.0)
+                for s in range(slots):
+                    hit = (codes_ref[s, x, y] == offset) & (s < counts_ref[x, y])
+                    w = w + jnp.where(hit, weights_ref[s, x, y], 0.0)
+                wt[offset, x * by + y] = w
+
     for copy in own:
         copy.wait()
     for x in range(bx):
@@ -275,10 +286,8 @@
         fac_ref[i // by, i % by] = gs[i].astype(fac_ref.dtype)
 
 
-def sum_kernel(fac_ref, v_ref, codes_ref, counts_ref, weights_ref, out_ref, img, loc, px, py, pc, rx, ry, rc, wt,
-               send_sem, recv_sem):
+def sum_kernel(fac_ref, v_ref, wt, out_ref, img, loc, px, py, pc, rx, ry, rc, send_sem, recv_sem):
     bx, by = fac_ref.shape[:2]
-    slots = codes_ref.shape[0]
     there, exists = neighbours()
     sends = [px.at[0], px.at[1], py.at[0], py.at[1]] + [pc.at[k] for k in range(4)]
     lands = [rx.at[0], rx.at[1], ry.at[0], ry.at[1]] + [rc.at[k] for k in range(4)]
@@ -295,12 +304,6 @@
     @pl.loop(0, by)
     def _(y):
         for x in range(bx):
-            for offset in range(9):
-                w = jnp.float32(0.0)
-                for s in range(slots):
-                    hit = (codes_ref[s, x, y] == offset) & (s < counts_ref[x, y])
-                    w = w + jnp.where(hit, weights_ref[s, x, y], 0.0)
-                wt[offset, x * by + y] = w
             img[x, y] = lax.dot_general(fac_ref[x, y], v_ref[x, y], (((0,), (0,)), ((), ())),
                                         preferred_element_type=jnp.float32)
 
@@ -371,11 +374,11 @@
     codes, weights = jnp.transpose(codes, (2, 0, 1)), jnp.transpose(weights, (2, 0, 1))
     padded = (bx + 2) * (by + 2)
     copies = 4 + 2 * bx + 2 * by
-    gram = pl.pallas_call(
+    gram, sums = pl.pallas_call(
         gram_kernel,
-        out_shape=jax.ShapeDtypeStruct((bx, by, order, order), f32),
-        in_specs=[anyspace, vmem, vmem, smem, smem],
-        out_specs=vmem,
+        out_shape=(jax.ShapeDtypeStruct((bx, by, order, order), f32), jax.ShapeDtypeStruct((9, bx * by), f32)),
+        in_specs=[anyspace, vmem, vmem, smem, smem, smem],
+        out_specs=(vmem, smem),
         scratch_shapes=[
             pltpu.VMEM((padded, coupling, order), bf16),
             pltpu.VMEM((padded, order, coupling), bf16),
@@ -384,7 +387,7 @@
         ],
         compiler_params=pltpu.CompilerParams(collective_id=0, has_side_effects=True),
         name="gram",
-    )(coeffs, permit, shift_diag, codes, counts)
+    )(coeffs, permit, shift_diag, codes, counts, weights)
     fac = pl.pallas_call(
         factor_kernel,
         out_shape=jax.ShapeDtypeStruct((bx, by, order, order), bf16),
@@ -401,18 +404,17 @@
     applied = pl.pallas_call(
         sum_kernel,
         out_shape=jax.ShapeDtypeStruct((bx, by, order, nv), bf16),
-        in_specs=[vmem, vmem, smem, smem, smem],
+        in_specs=[vmem, vmem, smem],
         out_specs=vmem,
         scratch_shapes=[
             pltpu.VMEM((bx, by, order, nv), f32),
             pltpu.VMEM((bx, by, order, nv), f32),
             *edges, *edges,
-            pltpu.SMEM((9, bx * by), f32),
             pltpu.SemaphoreType.DMA((8,)), pltpu.SemaphoreType.DMA((8,)),
         ],
         compiler_params=pltpu.CompilerParams(collective_id=1, has_side_effects=True),
         name="sums",
-    )(fac, vectors, codes, counts, weights)
+    )(fac, vectors, sums)
     return fac, applied
 
 

time: 55.1 us -> 53.8 us (0.976)
  Pallas kernels: 52.2 us -> 50.9 us
    pallas_call x1, Pallas kernels: 15.1 us -> 13.7 us  [local(): pl.pallas_call(sum_kernel, out_shape=jax.ShapeDtypeStruct((bx, by, order,...]
where the time goes in v6:
time: 53.8 us; the launch traced here: 53.5 us
  Pallas kernels  50.9 us (95%)
  local copies, waits for them, and re-layouts  1.89 us (4%)
  between operations  0.65 us (1%)
    pallas_call x1, Pallas kernels, local(): pl.pallas_call(gram_kernel, out_shape=(jax.ShapeDtypeStruct((bx, by, orde...  22.4 us
    pallas_call x1, Pallas kernels, local(): pl.pallas_call(factor_kernel, out_shape=jax.ShapeDtypeStruct((bx, by, ord...  14.8 us
    pallas_call x1, Pallas kernels, local(): pl.pallas_call(sum_kernel, out_shape=jax.ShapeDtypeStruct((bx, by, order,...  13.7 us
    unnamed x1, local copies, waits for them, and re-layouts  1.89 us

profile of v6, /device:TPU:4, one launch (start us, length us, event | category | flops | bytes accessed | tf_op | source)
XLA Modules:
  0.0 53.5 jit_solution(15650402568262015923)
XLA Ops:
  0.6 22.4 %gram.1 = (f32[2,8,128,128]{3,2,1,0:T(8,128)}, f32[9,16]{1,0:T(8,128)}) custom-call(bf16[2,8,256,128]{3,2,1,0:T(8,128)(2,1)} %c_ref.1, f32[2,8,256]{2,1,0:T(8,128)} %permit_ref.1, f32[2,8,128]{2,1,0:T(8,128)} %shift_ref.1, s32[6,2,8]{2,1,0:T(2,128)} %bitcast.2, s32[2,8]{1,0:T(2,128)} %counts_ref.1, f32[6,2,8]{2,1,0:T(2,128)} %bitcast.3), custom_call_target="tpu_custom_call" | custom-call | tf_op jit(solution)/shard_map/gram/pallas_call | solution.py:377
  23.1 14.8 %factor.1.fac_ref = bf16[2,8,128,128]{3,2,1,0:T(8,128)(2,1)} custom-call(f32[2,8,128,128]{3,2,1,0:T(8,128)} %get-tuple-element.4.gram_ref), custom_call_target="tpu_custom_call" | custom-call | tf_op jit(solution)/shard_map/factor/pallas_call | solution.py:391
  37.9 13.7 %sums.1 = bf16[2,8,128,128]{3,2,1,0:T(8,128)(2,1)} custom-call(bf16[2,8,128,128]{3,2,1,0:T(8,128)(2,1)} %factor.1.fac_ref, bf16[2,8,128,128]{3,2,1,0:T(8,128)(2,1)} %v_ref.1, f32[9,16]{1,0:T(8,128)} %get-tuple-element.5.wt), custom_call_target="tpu_custom_call" | custom-call | tf_op jit(solution)/shard_map/sums/pallas_call | solution.py:404
  51.6 1.9 %copy.10 = bf16[2,8,128,128]{3,2,1,0:T(8,128)(2,1)} copy(bf16[2,8,128,128]{3,2,1,0:T(8,128)(2,1)} %sums.1) | data formatting | bytes 1048576
